TPU v7x, 32 devices: a whole 2x2x4 slice. The times are simulated.
32 devices in a mesh: dp: 2 (over y), row: 4 (over z), col: 4 (over x, core).
Axes of the slice: x: 2, y: 2, z: 4, core: 2. Of those that a mesh axis runs over, the one named last changes fastest.
Arguments:
- residual_in: float32 [2, 8192, 1024], P(None, ('dp', 'row'), 'col'), may hold values from -57 to 57
- encoder_out: float32 [2, 8000, 1024], P(None, ('dp', 'row'), 'col'), may hold values from -6 to 6
- prefix_len: int32 [2, 8], P(None, ('dp', 'row')), may hold values from 102 to 512
- bucket_table: int32 [2047], replicated, may hold values from 0 to 31
- cotangent: float32 [2, 8192, 1024], P(None, ('dp', 'row'), 'col'), may hold values from -6 to 6
- norm_self: float32 [1024], P('col'), may hold values from 0.5 to 1.5
- norm_cross: float32 [1024], P('col'), may hold values from 0.5 to 1.5
- norm_ffn: float32 [1024], P('col'), may hold values from 0.5 to 1.5
- self_query: float32 [1024, 1024], P('row', 'col'), may hold values from -0.0625 to 0.0625
- self_key: float32 [1024, 1024], P('row', 'col'), may hold values from -0.1875 to 0.1875
- self_value: float32 [1024, 1024], P('row', 'col'), may hold values from -0.1875 to 0.1875
- self_out: float32 [1024, 1024], P('col', 'row'), may hold values from -0.375 to 0.375
- cross_query: float32 [1024, 1024], P('row', 'col'), may hold values from -0.046875 to 0.046875
- cross_key: float32 [1024, 1024], P('row', 'col'), may hold values from -0.1875 to 0.1875
- cross_value: float32 [1024, 1024], P('row', 'col'), may hold values from -0.1875 to 0.1875
- cross_out: float32 [1024, 1024], P('col', 'row'), may hold values from -0.375 to 0.375
- ffn_in: float32 [1024, 4096], P('row', 'col'), may hold values from -0.1875 to 0.1875
- ffn_out: float32 [4096, 1024], P('col', 'row'), may hold values from -0.125 to 0.125
- rel_bias: float32 [32, 16], P('row', 'col'), may hold values from -4 to 4
Outputs:
- layer_out: float32 [2, 8192, 1024], P(None, ('dp', 'row'), 'col')
- grad_residual: float32 [2, 8192, 1024], P(None, ('dp', 'row'), 'col')
- grad_encoder: float32 [2, 8000, 1024], P(None, ('dp', 'row'), 'col')
- grad_norm_self: float32 [1024], P('col')
- grad_norm_cross: float32 [1024], P('col')
- grad_norm_ffn: float32 [1024], P('col')
- grad_self_query: float32 [1024, 1024], P(('dp', 'row'), 'col')
- grad_self_key: float32 [1024, 1024], P(('dp', 'row'), 'col')
- grad_self_value: float32 [1024, 1024], P(('dp', 'row'), 'col')
- grad_self_out: float32 [1024, 1024], P('col', ('dp', 'row'))
- grad_cross_query: float32 [1024, 1024], P(('dp', 'row'), 'col')
- grad_cross_key: float32 [1024, 1024], P(('dp', 'row'), 'col')
- grad_cross_value: float32 [1024, 1024], P(('dp', 'row'), 'col')
- grad_cross_out: float32 [1024, 1024], P('col', ('dp', 'row'))
- grad_ffn_in: float32 [1024, 4096], P(('dp', 'row'), 'col')
- grad_ffn_out: float32 [4096, 1024], P('col', ('dp', 'row'))
- grad_rel_bias: float32 [32, 16], P(('dp', 'row'), 'col')
Inputs may be any that keep to these rules, and one draw needn't show every extreme that they name: The first prefix_len[m, s] tokens of a sequence attend to each other both ways.
All inputs are finite; a program needn't handle non-finite values.
Results may differ from a plain program's by a relative error of at most 0.029.
Values may be sent and summed in bfloat16 or wider, within the bound.
No kernel may reach another device: no remote copies, remote signals or barrier semaphores. Data moves between devices by JAX's collectives and lax.ppermute only.
A program may use at most 832 MiB of HBM per device.

v0:
```python
import jax
import jax.numpy as jnp
from jax import lax
from jax.sharding import PartitionSpec as P

NEG_FILL = -1000000000.0


def project(left, right):
    return jnp.dot(left, right, preferred_element_type=jnp.float32)


def project_back(left, right):
    return lax.dot_general(
        left, right, (((1,), (1,)), ((), ())), preferred_element_type=jnp.float32
    )


def project_left(left, right):
    return lax.dot_general(
        left, right, (((0,), (0,)), ((), ())), preferred_element_type=jnp.float32
    )


def smooth_act(values):
    return jax.nn.gelu(values, approximate=True)


def attention_scores(queries, key_rows, pos_bias, allowed):
    scores = jnp.einsum("qhe,khe->hqk", queries, key_rows, preferred_element_type=jnp.float32)
    if pos_bias is None:
        return scores
    return jnp.where(allowed[None], scores + pos_bias, NEG_FILL)


def attend_forward(queries, key_rows, value_rows, pos_bias, allowed):
    scores = attention_scores(queries, key_rows, pos_bias, allowed)
    row_max = jnp.max(scores, axis=2, keepdims=True)
    exp_scores = jnp.exp(scores - row_max)
    row_total = jnp.sum(exp_scores, axis=2, keepdims=True)
    attn_probs = (exp_scores / row_total).astype(jnp.bfloat16)
    mixed = jnp.einsum("hqk,khe->qhe", attn_probs, value_rows, preferred_element_type=jnp.float32)
    return (mixed.astype(jnp.bfloat16), row_max + jnp.log(row_total))


def attend_backward(queries, key_rows, value_rows, pos_bias, allowed, log_total, grad_mixed):
    scores = attention_scores(queries, key_rows, pos_bias, allowed)
    attn_probs = jnp.exp(scores - log_total)
    grad_values = jnp.einsum(
        "hqk,qhe->khe",
        attn_probs.astype(jnp.bfloat16),
        grad_mixed,
        preferred_element_type=jnp.float32,
    )
    grad_probs = jnp.einsum(
        "qhe,khe->hqk", grad_mixed, value_rows, preferred_element_type=jnp.float32
    )
    grad_scores = attn_probs * (
        grad_probs - jnp.sum(attn_probs * grad_probs, axis=2, keepdims=True)
    )
    grad_scores_low = grad_scores.astype(jnp.bfloat16)
    grad_queries = jnp.einsum(
        "hqk,khe->qhe", grad_scores_low, key_rows, preferred_element_type=jnp.float32
    )
    grad_keys = jnp.einsum(
        "hqk,qhe->khe", grad_scores_low, queries, preferred_element_type=jnp.float32
    )
    return (
        grad_queries.astype(jnp.bfloat16),
        grad_keys.astype(jnp.bfloat16),
        grad_values.astype(jnp.bfloat16),
        grad_scores_low,
    )


def diagonal_sums(square):
    head_count = square.shape[0]
    length = square.shape[1]
    flipped = square[:, ::-1, :]
    padded = jnp.pad(flipped, ((0, 0), (0, 0), (0, length)))
    flattened = padded.reshape(head_count, 2 * length * length)[:, : length * (2 * length - 1)]
    return jnp.sum(flattened.reshape(head_count, length, 2 * length - 1), axis=1)


def normalize(resid_rows, gain_vec):
    model_width = resid_rows.shape[1] * lax.axis_size("col")
    square_sum = lax.psum(jnp.sum(resid_rows * resid_rows, axis=1), "col")
    inv_scale = lax.rsqrt(square_sum / model_width + 1e-06)
    normed = lax.all_gather(
        (resid_rows * inv_scale[:, None] * gain_vec).astype(jnp.bfloat16), "col", axis=1, tiled=True
    )
    return (normed, inv_scale)


def norm_backward(grad_part, resid_rows, inv_scale, gain_vec):
    model_width = resid_rows.shape[1] * lax.axis_size("col")
    grad_normed = lax.psum_scatter(grad_part, "col", scatter_dimension=1, tiled=True)
    scaled = grad_normed * gain_vec
    inner_sum = lax.psum(jnp.sum(scaled * resid_rows, axis=1), "col")
    grad_resid = (
        inv_scale[:, None] * scaled
        - resid_rows * (inv_scale * inv_scale * inv_scale * inner_sum / model_width)[:, None]
    )
    grad_gain = jnp.sum(grad_normed * resid_rows * inv_scale[:, None], axis=0)
    return (grad_resid, grad_gain)


def branch_sum(partial_rows):
    return lax.psum_scatter(partial_rows, "col", scatter_dimension=1, tiled=True)


def branch_grad(grad_rows):
    return lax.all_gather(grad_rows.astype(jnp.bfloat16), "col", axis=1, tiled=True)


def body(
    residual_in,
    encoder_out,
    prefix_len,
    bucket_table,
    cotangent,
    norm_self,
    norm_cross,
    norm_ffn,
    self_query,
    self_key,
    self_value,
    self_out,
    cross_query,
    cross_key,
    cross_value,
    cross_out,
    ffn_in,
    ffn_out,
    rel_bias,
):
    low_type = jnp.bfloat16
    micro_count = residual_in.shape[0]
    seq_count = prefix_len.shape[1]
    seq_len = (bucket_table.shape[0] + 1) // 2
    token_rows = seq_count * seq_len
    head_count = rel_bias.shape[1]
    inner_width = self_query.shape[1]
    head_size = inner_width // head_count
    gathered = (
        lax.all_gather(self_query.astype(low_type), "row", axis=0, tiled=True),
        lax.all_gather(self_key.astype(low_type), "row", axis=0, tiled=True),
        lax.all_gather(self_value.astype(low_type), "row", axis=0, tiled=True),
        lax.all_gather(self_out.astype(low_type), "row", axis=1, tiled=True),
        lax.all_gather(cross_query.astype(low_type), "row", axis=0, tiled=True),
        lax.all_gather(cross_key.astype(low_type), "row", axis=0, tiled=True),
        lax.all_gather(cross_value.astype(low_type), "row", axis=0, tiled=True),
        lax.all_gather(cross_out.astype(low_type), "row", axis=1, tiled=True),
        lax.all_gather(ffn_in.astype(low_type), "row", axis=0, tiled=True),
        lax.all_gather(ffn_out.astype(low_type), "row", axis=1, tiled=True),
        lax.all_gather(rel_bias.astype(low_type), "row", axis=0, tiled=True),
    )
    full_self_query, full_self_key, full_self_value, full_self_out = (
        gathered[0],
        gathered[1],
        gathered[2],
        gathered[3],
    )
    full_cross_query, full_cross_key, full_cross_value, full_cross_out = (
        gathered[4],
        gathered[5],
        gathered[6],
        gathered[7],
    )
    full_ffn_in, full_ffn_out, full_bias = (gathered[8], gathered[9], gathered[10])
    model_width = full_self_query.shape[0]
    ffn_width = full_ffn_in.shape[1]
    qkv_weight = jnp.concatenate((full_self_query, full_self_key, full_self_value), axis=1)
    kv_weight = jnp.concatenate((full_cross_key, full_cross_value), axis=1)
    bucket_ids = jnp.arange(full_bias.shape[0], dtype=jnp.int32)
    bucket_onehot = (bucket_table[:, None] == bucket_ids[None, :]).astype(jnp.float32)
    distance_bias = jnp.dot(
        bucket_onehot, full_bias.astype(jnp.float32), precision=lax.Precision.HIGHEST
    ).T
    places = jnp.arange(seq_len, dtype=jnp.int32)
    offsets = places[None, :] - places[:, None] + seq_len - 1
    pos_bias = jnp.take(distance_bias, offsets, axis=1)
    causal = places[None, :] <= places[:, None]

    def split_heads(flat_rows, count):
        return flat_rows.reshape(seq_count, count, head_count, head_size)

    outputs = []
    grad_inputs = []
    grad_memory = []
    running = [
        jnp.zeros((model_width, 3 * inner_width), jnp.float32),
        jnp.zeros((inner_width, model_width), jnp.float32),
        jnp.zeros((model_width, inner_width), jnp.float32),
        jnp.zeros((model_width, 2 * inner_width), jnp.float32),
        jnp.zeros((inner_width, model_width), jnp.float32),
        jnp.zeros((model_width, ffn_width), jnp.float32),
        jnp.zeros((ffn_width, model_width), jnp.float32),
        jnp.zeros((head_count, seq_len, seq_len), jnp.float32),
    ]
    gain_sums = [jnp.zeros(norm_self.shape, jnp.float32) for _ in range(3)]
    for micro_step in range(micro_count):
        resid_zero = residual_in[micro_step]
        normed_one, scale_one = normalize(resid_zero, norm_self)
        qkv_rows = (
            project(normed_one, qkv_weight)
            .astype(low_type)
            .reshape(seq_count, seq_len, 3, head_count, head_size)
        )
        queries, key_rows, value_rows = (qkv_rows[:, :, 0], qkv_rows[:, :, 1], qkv_rows[:, :, 2])

        def self_forward(pieces):
            query_seq, key_seq, value_seq, cut_len = pieces
            allowed = causal | (places[None, :] < cut_len)
            return attend_forward(query_seq, key_seq, value_seq, pos_bias, allowed)

        self_mix, self_total = lax.map(
            self_forward, (queries, key_rows, value_rows, prefix_len[micro_step])
        )
        self_flat = self_mix.reshape(token_rows, inner_width)
        resid_one = resid_zero + branch_sum(project(self_flat, full_self_out))
        normed_two, scale_two = normalize(resid_one, norm_cross)
        cross_queries = split_heads(project(normed_two, full_cross_query).astype(low_type), seq_len)
        memory_rows = lax.all_gather(
            encoder_out[micro_step].astype(low_type), "col", axis=1, tiled=True
        )
        memory_len = memory_rows.shape[0] // seq_count
        kv_rows = (
            project(memory_rows, kv_weight)
            .astype(low_type)
            .reshape(seq_count, memory_len, 2, head_count, head_size)
        )
        cross_keys, cross_values = (kv_rows[:, :, 0], kv_rows[:, :, 1])

        def cross_forward(pieces):
            query_seq, key_seq, value_seq = pieces
            return attend_forward(query_seq, key_seq, value_seq, None, None)

        cross_mix, cross_total = lax.map(cross_forward, (cross_queries, cross_keys, cross_values))
        cross_flat = cross_mix.reshape(token_rows, inner_width)
        resid_two = resid_one + branch_sum(project(cross_flat, full_cross_out))
        normed_three, scale_three = normalize(resid_two, norm_ffn)
        ffn_pre = project(normed_three, full_ffn_in)
        act_values, act_pull = jax.vjp(smooth_act, ffn_pre)
        ffn_act = act_values.astype(low_type)
        outputs.append(resid_two + branch_sum(project(ffn_act, full_ffn_out)))
        grad_top = cotangent[micro_step]
        grad_rows = branch_grad(grad_top)
        running[6] = running[6] + project_left(ffn_act, grad_rows)
        grad_pre = act_pull(project_back(grad_rows, full_ffn_out))[0].astype(low_type)
        running[5] = running[5] + project_left(normed_three, grad_pre)
        grad_two, gain_part = norm_backward(
            project_back(grad_pre, full_ffn_in), resid_two, scale_three, norm_ffn
        )
        gain_sums[2] = gain_sums[2] + gain_part
        grad_two = grad_two + grad_top
        grad_rows = branch_grad(grad_two)
        running[4] = running[4] + project_left(cross_flat, grad_rows)
        grad_cross_mix = split_heads(
            project_back(grad_rows, full_cross_out).astype(low_type), seq_len
        )

        def cross_backward(pieces):
            query_seq, key_seq, value_seq, total_seq, grad_seq = pieces
            grad_query, grad_key, grad_value, grad_scores_low = attend_backward(
                query_seq, key_seq, value_seq, None, None, total_seq, grad_seq
            )
            return (grad_query, grad_key, grad_value)

        cross_grad_query, cross_grad_key, cross_grad_value = lax.map(
            cross_backward, (cross_queries, cross_keys, cross_values, cross_total, grad_cross_mix)
        )
        cross_grad_flat = cross_grad_query.reshape(token_rows, inner_width)
        grad_kv = jnp.stack((cross_grad_key, cross_grad_value), axis=2).reshape(
            seq_count * memory_len, 2 * inner_width
        )
        running[2] = running[2] + project_left(normed_two, cross_grad_flat)
        running[3] = running[3] + project_left(memory_rows, grad_kv)
        grad_memory.append(
            lax.psum_scatter(
                project_back(grad_kv, kv_weight).astype(jnp.bfloat16),
                "col",
                scatter_dimension=1,
                tiled=True,
            ).astype(jnp.float32)
        )
        grad_one, gain_part = norm_backward(
            project_back(cross_grad_flat, full_cross_query), resid_one, scale_two, norm_cross
        )
        gain_sums[1] = gain_sums[1] + gain_part
        grad_one = grad_one + grad_two
        grad_rows = branch_grad(grad_one)
        running[1] = running[1] + project_left(self_flat, grad_rows)
        grad_self_mix = split_heads(
            project_back(grad_rows, full_self_out).astype(low_type), seq_len
        )

        def self_backward(square_sum, pieces):
            query_seq, key_seq, value_seq, cut_len, total_seq, grad_seq = pieces
            allowed = causal | (places[None, :] < cut_len)
            grad_query, grad_key, grad_value, grad_scores_low = attend_backward(
                query_seq, key_seq, value_seq, pos_bias, allowed, total_seq, grad_seq
            )
            return (
                square_sum + grad_scores_low.astype(jnp.float32),
                (grad_query, grad_key, grad_value),
            )

        bias_square, (self_grad_query, self_grad_key, self_grad_value) = lax.scan(
            self_backward,
            running[7],
            (queries, key_rows, value_rows, prefix_len[micro_step], self_total, grad_self_mix),
        )
        running[7] = bias_square
        grad_qkv = jnp.stack((self_grad_query, self_grad_key, self_grad_value), axis=2).reshape(
            token_rows, 3 * inner_width
        )
        running[0] = running[0] + project_left(normed_one, grad_qkv)
        grad_zero, gain_part = norm_backward(
            project_back(grad_qkv, qkv_weight), resid_zero, scale_one, norm_self
        )
        gain_sums[0] = gain_sums[0] + gain_part
        grad_inputs.append(grad_zero + grad_one)
    bias_grad = jnp.dot(
        bucket_onehot.T, diagonal_sums(running[7]).T, precision=lax.Precision.HIGHEST
    )
    weight_grads = (
        lax.psum_scatter(
            running[0][:, :inner_width].astype(jnp.bfloat16),
            ("dp", "row"),
            scatter_dimension=0,
            tiled=True,
        ).astype(jnp.float32),
        lax.psum_scatter(
            running[0][:, inner_width : 2 * inner_width].astype(jnp.bfloat16),
            ("dp", "row"),
            scatter_dimension=0,
            tiled=True,
        ).astype(jnp.float32),
        lax.psum_scatter(
            running[0][:, 2 * inner_width :].astype(jnp.bfloat16),
            ("dp", "row"),
            scatter_dimension=0,
            tiled=True,
        ).astype(jnp.float32),
        lax.psum_scatter(
            running[1].astype(jnp.bfloat16), ("dp", "row"), scatter_dimension=1, tiled=True
        ).astype(jnp.float32),
        lax.psum_scatter(
            running[2].astype(jnp.bfloat16), ("dp", "row"), scatter_dimension=0, tiled=True
        ).astype(jnp.float32),
        lax.psum_scatter(
            running[3][:, :inner_width].astype(jnp.bfloat16),
            ("dp", "row"),
            scatter_dimension=0,
            tiled=True,
        ).astype(jnp.float32),
        lax.psum_scatter(
            running[3][:, inner_width:].astype(jnp.bfloat16),
            ("dp", "row"),
            scatter_dimension=0,
            tiled=True,
        ).astype(jnp.float32),
        lax.psum_scatter(
            running[4].astype(jnp.bfloat16), ("dp", "row"), scatter_dimension=1, tiled=True
        ).astype(jnp.float32),
        lax.psum_scatter(
            running[5].astype(jnp.bfloat16), ("dp", "row"), scatter_dimension=0, tiled=True
        ).astype(jnp.float32),
        lax.psum_scatter(
            running[6].astype(jnp.bfloat16), ("dp", "row"), scatter_dimension=1, tiled=True
        ).astype(jnp.float32),
        lax.psum_scatter(
            bias_grad.astype(jnp.bfloat16), ("dp", "row"), scatter_dimension=0, tiled=True
        ).astype(jnp.float32),
    )
    gain_grads = lax.psum((gain_sums[0], gain_sums[1], gain_sums[2]), ("dp", "row"))
    return (
        jnp.stack(outputs),
        jnp.stack(grad_inputs),
        jnp.stack(grad_memory),
        gain_grads[0],
        gain_grads[1],
        gain_grads[2],
        weight_grads[0],
        weight_grads[1],
        weight_grads[2],
        weight_grads[3],
        weight_grads[4],
        weight_grads[5],
        weight_grads[6],
        weight_grads[7],
        weight_grads[8],
        weight_grads[9],
        weight_grads[10],
    )


def solution(mesh):
    in_specs = (
        P(None, ("dp", "row"), "col"),
        P(None, ("dp", "row"), "col"),
        P(None, ("dp", "row")),
        P(),
        P(None, ("dp", "row"), "col"),
        P("col"),
        P("col"),
        P("col"),
        P("row", "col"),
        P("row", "col"),
        P("row", "col"),
        P("col", "row"),
        P("row", "col"),
        P("row", "col"),
        P("row", "col"),
        P("col", "row"),
        P("row", "col"),
        P("col", "row"),
        P("row", "col"),
    )
    out_specs = (
        P(None, ("dp", "row"), "col"),
        P(None, ("dp", "row"), "col"),
        P(None, ("dp", "row"), "col"),
        P("col"),
        P("col"),
        P("col"),
        P(("dp", "row"), "col"),
        P(("dp", "row"), "col"),
        P(("dp", "row"), "col"),
        P("col", ("dp", "row")),
        P(("dp", "row"), "col"),
        P(("dp", "row"), "col"),
        P(("dp", "row"), "col"),
        P("col", ("dp", "row")),
        P(("dp", "row"), "col"),
        P("col", ("dp", "row")),
        P(("dp", "row"), "col"),
    )
    return jax.shard_map(body, mesh=mesh, in_specs=in_specs, out_specs=out_specs, check_vma=False)
```

profile of v0, /device:TPU:0, one launch (start us, length us, event | category | flops | bytes accessed | tf_op | source)
XLA Modules:
  0.0 5987.7 jit_solution(13420544991643633530)
XLA Ops:
  26.7 11.2 all-gather.2
  44.5 3771.1 %gather_fusion = f32[1048576,4]{1,0:T(8,128)} fusion(f32[4,2047]{0,1:T(8,128)S(1)} %copy.70, s32[1048576]{0:T(1024)} %broadcast_clamp_fusion), kind=kCustom, calls=%fused_computation | custom fusion | bytes 37748736 | tf_op jit(solution)/shard_map/jit(_take)/gather | solution.py:182
  3815.6 282.2 %copy.72 = f32[1024,1024,4]{0,1,2:T(8,128)} copy(f32[1024,1024,4]{2,1,0:T(8,128)} %bitcast.8) | data formatting | bytes 33554432 | tf_op jit(solution)/shard_map/jit(_take)/gather | solution.py:182
  4097.8 15.0 all_gather.76
  4113.8 16.6 all_gather.77
  4130.4 15.6 all_gather.78
  4147.6 14.9 all_gather.80
  4168.3 12.1 fusion.159
  4205.3 12.8 fusion.160
  4241.3 47.1 reduce-scatter.41.cloned.1.call-done
  4303.3 15.6 all_gather.81
  4319.0 17.3 all_gather.82
  4336.3 15.4 all_gather.85
  4351.7 16.3 all_gather.86
  4450.9 44.9 reduce-scatter.43.cloned.1.call-done
  4519.7 40.6 all-gather.26.cloned.1.call-done
  4560.3 23.7 all-gather.24.cloned.1.call-done
  4584.0 10.0 fusion.32
  4600.5 43.8 reduce-scatter.47.cloned.1.call-done
  4648.3 20.9 all-gather.42.cloned.1.call-done
  4675.8 18.2 all-gather.34.cloned.1.call-done
  4694.0 10.0 fusion.39
  4726.1 28.2 reduce-scatter.53.cloned.1.call-done
  4762.7 38.5 reduce-scatter.39.cloned.1.call-done
  4801.2 47.2 reduce-scatter.45.cloned.1.call-done
  4854.3 22.4 all-gather.38.cloned.1.call-done
  4879.9 16.1 multiply_reduce_fusion.3
  4914.3 18.1 multiply_reduce_fusion.2
  4955.3 47.2 reduce-scatter.55.cloned.1.call-done
  5089.9 10.9 multiply_reduce_fusion.1
  5103.1 11.2 multiply_reduce_fusion
  5114.3 34.6 convert_add_fusion
  5219.0 49.8 reduce-scatter.75.cloned.1.call-done
  5270.5 62.8 %reduce-scatter.77.cloned.1.call-done = bf16[128,256]{1,0:T(8,128)(2,1)} async-done(((bf16[1024,256]{1,0:T(8,128)(2,1)}), bf16[128,256]{1,0:T(8,128)(2,1)}) %reduce-scatter.77.cloned.1.call-update) | async-done | bytes 65552
  5335.0 62.6 %reduce-scatter.79.cloned.1.call-done = bf16[128,256]{1,0:T(8,128)(2,1)} async-done(((bf16[1024,256]{1,0:T(8,128)(2,1)}), bf16[128,256]{1,0:T(8,128)(2,1)}) %reduce-scatter.79.cloned.1.call-update) | async-done | bytes 65552
  5399.2 62.9 %reduce-scatter.69.cloned.1.call-done = bf16[128,256]{1,0:T(8,128)(2,1)} async-done(((bf16[1024,256]{1,0:T(8,128)(2,1)}), bf16[128,256]{1,0:T(8,128)(2,1)}) %reduce-scatter.69.cloned.1.call-update) | async-done | bytes 65552 | tf_op jit(solution)/shard_map/reduce_scatter | solution.py:349
  5463.6 31.8 reduce-scatter.61.cloned.1.call-done
  5495.4 33.9 reduce-scatter.59.cloned.1.call-done
  5532.0 134.4 %rev.3 = f32[4,1024,1024]{1,2,0:T(8,128)} reverse(f32[4,1024,1024]{1,2,0:T(8,128)} %get-tuple-element.333), dimensions={1} | reverse | bytes 33554432 | tf_op jit(solution)/shard_map/rev | solution.py:79
  5666.4 16.5 copy.106
  5682.9 18.9 pad_bitcast_fusion
  5701.9 38.0 copy.108
  5739.8 23.7 slice.124
  5763.5 95.1 %reshape.335 = f32[8384512]{0:T(1024)} reshape(f32[4,2096128]{1,0:T(4,128)} %slice.124) | data formatting | bytes 67076096
  5858.6 49.7 reshape.310
  5908.3 12.4 reduce_sum.277
  5921.8 21.9 all-reduce.1
  5962.2 17.8 all-reduce.2
  (520 shorter events, 487.2 us)
Async XLA Ops:
  8.0 4156.3 %all-gather.20.cloned.1.call-start = ((), (), s32[]{:S(2)}) async-start(), calls=%async_computation.24 | async-start | bytes 2621440 | tf_op jit(solution)/shard_map/all_gather | solution.py:89
  22.0 4178.8 %all-gather.30.cloned.1.call-start = ((), (), s32[]{:S(2)}) async-start(), calls=%async_computation.32 | async-start | bytes 2621440 | tf_op jit(solution)/shard_map/all_gather | solution.py:89
  22.8 4218.6 %reduce-scatter.35.cloned.1.call-start = ((), (), s32[]{:S(2)}) async-start(), calls=%async_computation.25 | async-start | bytes 5242880 | tf_op jit(solution)/shard_map/reduce_scatter | solution.py:109
  3815.6 282.2 %copy-start.51 = (f32[256,256]{1,0:T(8,128)S(1)}, f32[256,256]{1,0:T(8,128)}, u32[]{:S(2)}) copy-start(f32[256,256]{1,0:T(8,128)} %param.27) | copy-start | bytes 786436
  3815.6 298.1 %copy-start.52 = (f32[256,256]{1,0:T(8,128)S(1)}, f32[256,256]{1,0:T(8,128)}, u32[]{:S(2)}) copy-start(f32[256,256]{1,0:T(8,128)} %param.28) | copy-start | bytes 786436
  3815.6 314.8 %copy-start.53 = (f32[256,256]{1,0:T(8,128)S(1)}, f32[256,256]{1,0:T(8,128)}, u32[]{:S(2)}) copy-start(f32[256,256]{1,0:T(8,128)} %param.29) | copy-start | bytes 786436
  4162.6 71.1 %copy-start.10 = (bf16[256,1024]{1,0:T(8,128)(2,1)}, bf16[256,1024]{1,0:T(8,128)(2,1)S(1)}, u32[]{:S(2)}) copy-start(bf16[256,1024]{1,0:T(8,128)(2,1)S(1)} %all_gather.80) | copy-start | bytes 1572868
  4199.5 88.9 %reduce-scatter.41.cloned.1.call-start = ((), (), s32[]{:S(2)}) async-start(), calls=%async_computation.33 | async-start | bytes 5242880 | tf_op jit(solution)/shard_map/reduce_scatter | solution.py:109
  4237.2 130.7 %all-gather.48.cloned.1.call-start = ((), (), s32[]{:S(2)}) async-start(), calls=%async_computation.57 | async-start | bytes 2560000 | tf_op jit(solution)/shard_map/all_gather | solution.py:224
  4240.2 133.1 %all-gather.22.cloned.1.call-start = ((), (), s32[]{:S(2)}) async-start(), calls=%async_computation.26 | async-start | bytes 2621440 | tf_op jit(solution)/shard_map/all_gather | solution.py:89
  4300.4 103.2 %all-gather.50.cloned.1.call-start = ((), (), s32[]{:S(2)}) async-start(), calls=%async_computation.58 | async-start | bytes 2560000 | tf_op jit(solution)/shard_map/all_gather | solution.py:224
  4301.2 108.8 %all-gather.32.cloned.1.call-start = ((), (), s32[]{:S(2)}) async-start(), calls=%async_computation.34 | async-start | bytes 2621440 | tf_op jit(solution)/shard_map/all_gather | solution.py:89
  4373.2 75.3 %reduce-scatter.37.cloned.1.call-start = ((), (), s32[]{:S(2)}) async-start(), calls=%async_computation.27 | async-start | bytes 5242880 | tf_op jit(solution)/shard_map/reduce_scatter | solution.py:109
  4403.4 92.4 %reduce-scatter.43.cloned.1.call-start = ((), (), s32[]{:S(2)}) async-start(), calls=%async_computation.35 | async-start | bytes 5242880 | tf_op jit(solution)/shard_map/reduce_scatter | solution.py:109
  4440.4 66.8 %all-gather.28.cloned.1.call-start = ((), (), s32[]{:S(2)}) async-start(), calls=%async_computation.30 | async-start | bytes 2621440 | tf_op jit(solution)/shard_map/all_gather | solution.py:155
  4442.4 70.7 %all-gather.36.cloned.1.call-start = ((), (), s32[]{:S(2)}) async-start(), calls=%async_computation.38 | async-start | bytes 2621440 | tf_op jit(solution)/shard_map/all_gather | solution.py:113
  4445.3 115.0 %all-gather.26.cloned.1.call-start = ((), (), s32[]{:S(2)}) async-start(), calls=%async_computation.29 | async-start | bytes 2621440 | tf_op jit(solution)/shard_map/all_gather | solution.py:154
  4447.4 136.5 %all-gather.24.cloned.1.call-start = ((), (), s32[]{:S(2)}) async-start(), calls=%async_computation.28 | async-start | bytes 2621440 | tf_op jit(solution)/shard_map/all_gather | solution.py:89
  4506.9 137.4 %reduce-scatter.47.cloned.1.call-start = ((), (), s32[]{:S(2)}) async-start(), calls=%async_computation.39 | async-start | bytes 5242880 | tf_op jit(solution)/shard_map/reduce_scatter | solution.py:97
  4599.7 69.5 %all-gather.42.cloned.1.call-start = ((), (), s32[]{:S(2)}) async-start(), calls=%async_computation.44 | async-start | bytes 2621440 | tf_op jit(solution)/shard_map/all_gather | solution.py:113
  4600.5 93.5 %all-gather.34.cloned.1.call-start = ((), (), s32[]{:S(2)}) async-start(), calls=%async_computation.36 | async-start | bytes 2621440 | tf_op jit(solution)/shard_map/all_gather | solution.py:89
  4647.9 106.5 %reduce-scatter.53.cloned.1.call-start = ((), (), s32[]{:S(2)}) async-start(), calls=%async_computation.45 | async-start | bytes 5242880 | tf_op jit(solution)/shard_map/reduce_scatter | solution.py:97
  4709.8 91.4 %reduce-scatter.39.cloned.1.call-start = ((), (), s32[]{:S(2)}) async-start(), calls=%async_computation.31 | async-start | bytes 5242880 | tf_op jit(solution)/shard_map/reduce_scatter | solution.py:109
  4717.4 131.0 %reduce-scatter.45.cloned.1.call-start = ((), (), s32[]{:S(2)}) async-start(), calls=%async_computation.37 | async-start | bytes 5242880 | tf_op jit(solution)/shard_map/reduce_scatter | solution.py:109
  4726.1 150.6 %all-gather.38.cloned.1.call-start = ((), (), s32[]{:S(2)}) async-start(), calls=%async_computation.40 | async-start | bytes 2621440 | tf_op jit(solution)/shard_map/all_gather | solution.py:113
  4853.7 57.4 all-gather.44.cloned.1.call-start
  4854.2 101.0 %reduce-scatter.49.cloned.1.call-start = ((), (), s32[]{:S(2)}) async-start(), calls=%async_computation.41 | async-start | bytes 5242880 | tf_op jit(solution)/shard_map/reduce_scatter | solution.py:97
  4910.7 91.7 %reduce-scatter.55.cloned.1.call-start = ((), (), s32[]{:S(2)}) async-start(), calls=%async_computation.47 | async-start | bytes 5242880 | tf_op jit(solution)/shard_map/reduce_scatter | solution.py:97
  4947.0 64.2 %copy-start.78 = (f32[1024]{0:T(1024)S(1)}, f32[1024]{0:T(1024)}, u32[]{:S(2)}) copy-start(f32[1024]{0:T(1024)} %copy-done.77) | copy-start | bytes 12292
  4947.0 64.2 %copy-start.76 = (f32[1024]{0:T(1024)S(1)}, f32[1024]{0:T(1024)}, u32[]{:S(2)}) copy-start(f32[1024]{0:T(1024)} %copy-done.75) | copy-start | bytes 12292
  4947.1 140.3 %all-gather.40.cloned.1.call-start = ((), (), s32[]{:S(2)}) async-start(), calls=%async_computation.42 | async-start | bytes 2621440 | tf_op jit(solution)/shard_map/all_gather | solution.py:113
  5015.0 85.8 %all-gather.46.cloned.1.call-start = ((), (), s32[]{:S(2)}) async-start(), calls=%async_computation.48 | async-start | bytes 2621440 | tf_op jit(solution)/shard_map/all_gather | solution.py:113
  5015.6 198.1 %reduce-scatter.81.cloned.1.call-start = ((), (), s32[]{:S(2)}) async-start(), calls=%async_computation.63 | async-start | bytes 2359296
  5027.5 188.1 %reduce-scatter.71.cloned.1.call-start = ((), (), s32[]{:S(2)}) async-start(), calls=%async_computation.56 | async-start | bytes 2359296 | tf_op jit(solution)/shard_map/reduce_scatter | solution.py:367
  5036.3 232.4 %reduce-scatter.75.cloned.1.call-start = ((), (), s32[]{:S(2)}) async-start(), calls=%async_computation.60 | async-start | bytes 589824
  5066.6 266.7 %reduce-scatter.77.cloned.1.call-start = ((), (), s32[]{:S(2)}) async-start(), calls=%async_computation.61 | async-start | bytes 589824
  5067.7 329.9 %reduce-scatter.79.cloned.1.call-start = ((), (), s32[]{:S(2)}) async-start(), calls=%async_computation.62 | async-start | bytes 589824
  5075.6 386.4 %reduce-scatter.69.cloned.1.call-start = ((), (), s32[]{:S(2)}) async-start(), calls=%async_computation.55 | async-start | bytes 589824 | tf_op jit(solution)/shard_map/reduce_scatter | solution.py:349
  5079.2 416.2 %reduce-scatter.61.cloned.1.call-start = ((), (), s32[]{:S(2)}) async-start(), calls=%async_computation.51 | async-start | bytes 2560000 | tf_op jit(solution)/shard_map/reduce_scatter | solution.py:280
  5083.2 446.2 %reduce-scatter.59.cloned.1.call-start = ((), (), s32[]{:S(2)}) async-start(), calls=%async_computation.50 | async-start | bytes 2560000 | tf_op jit(solution)/shard_map/reduce_scatter | solution.py:280
  5087.3 857.0 %reduce-scatter.73.cloned.1.call-start = ((), (), s32[]{:S(2)}) async-start(), calls=%async_computation.59 | async-start | bytes 589824
  5189.6 756.3 %reduce-scatter.63.cloned.1.call-start = ((), (), s32[]{:S(2)}) async-start(), calls=%async_computation.52 | async-start | bytes 589824 | tf_op jit(solution)/shard_map/reduce_scatter | solution.py:328
  5198.4 749.0 %reduce-scatter.65.cloned.1.call-start = ((), (), s32[]{:S(2)}) async-start(), calls=%async_computation.53 | async-start | bytes 589824 | tf_op jit(solution)/shard_map/reduce_scatter | solution.py:334
  5199.2 749.7 %reduce-scatter.67.cloned.1.call-start = ((), (), s32[]{:S(2)}) async-start(), calls=%async_computation.54 | async-start | bytes 589824 | tf_op jit(solution)/shard_map/reduce_scatter | solution.py:340
  5199.8 750.7 %reduce-scatter.51.cloned.1.call-start = ((), (), s32[]{:S(2)}) async-start(), calls=%async_computation.43 | async-start | bytes 5242880 | tf_op jit(solution)/shard_map/reduce_scatter | solution.py:97
  5205.2 745.3 %reduce-scatter.57.cloned.1.call-start = ((), (), s32[]{:S(2)}) async-start(), calls=%async_computation.49 | async-start | bytes 5242880 | tf_op jit(solution)/shard_map/reduce_scatter | solution.py:97
  5217.5 314.5 %copy-start.88 = (f32[256]{0:T(256)S(1)}, f32[256]{0:T(256)}, u32[]{:S(2)}) copy-start(f32[256]{0:T(256)} %get-tuple-element.314) | copy-start | bytes 3076
  5217.5 314.5 %copy-start.89 = (f32[256]{0:T(256)S(1)}, f32[256]{0:T(256)}, u32[]{:S(2)}) copy-start(f32[256]{0:T(256)} %get-tuple-element.374) | copy-start | bytes 3076
  (115 other events, 1699.8 us)
Sparse Core Ops, SparseCore 0:
  22.1 23.1 all-gather.19
  47.4 22.8 all-gather.29
  4199.6 41.6 reduce-scatter.34
  4243.9 44.4 reduce-scatter.40
  4290.4 22.5 all-gather.47
  4315.0 22.8 all-gather.21
  4340.0 22.5 all-gather.49
  4373.4 23.3 all-gather.31
  4403.5 45.0 reduce-scatter.36
  4451.1 44.6 reduce-scatter.42
  4853.8 22.8 all-gather.37
  4878.7 22.8 all-gather.43
  5015.2 23.5 all-gather.39
  5040.1 22.8 all-gather.45
  5066.4 67.6 reduce-scatter.80
  5138.0 66.5 reduce-scatter.70
  5207.8 60.9 reduce-scatter.74
  5272.3 60.8 reduce-scatter.76
  5336.6 60.9 reduce-scatter.78
  5401.1 60.8 reduce-scatter.68
  5465.2 30.1 reduce-scatter.60
  5498.2 31.1 reduce-scatter.58
  5532.7 62.0 reduce-scatter.72
  5598.4 61.0 reduce-scatter.62
  5662.8 60.9 reduce-scatter.64
  5727.3 60.8 reduce-scatter.66
  5790.6 43.5 reduce-scatter.50
  5836.8 44.5 reduce-scatter.56
Sparse Core Ops, SparseCore 1:
  4443.0 46.8 all-gather.27
  4492.0 21.1 all-gather.35
  4514.7 45.5 all-gather.25
  4562.4 21.5 all-gather.23
  4599.8 44.4 reduce-scatter.46
  4646.5 22.7 all-gather.41
  4671.3 22.7 all-gather.33
  4709.9 44.4 reduce-scatter.52
  4756.8 44.4 reduce-scatter.38
  4803.9 44.4 reduce-scatter.44
  4910.8 44.4 reduce-scatter.48
  4958.0 44.4 reduce-scatter.54
where the time goes:
time: 6080 us; the launch traced here: 5990 us
  local copies, waits for them, and re-layouts  4480 us (74%)
  waiting for transfers between devices  748 us (12%)
  matrix products  358 us (6%)
  blocking collectives  216 us (4%)
  other arithmetic  168 us (3%)
    gather x2, local copies, waits for them, and re-layouts, body(): pos_bias = jnp.take(distance_bias, offsets, axis=1)  4050 us
    unnamed x268, local copies, waits for them, and re-layouts  205 us
    unnamed x45, waiting for transfers between devices  180 us
    reduce_scatter x6, waiting for transfers between devices, branch_sum(): lax.psum_scatter(partial_rows, 'col', scatter_dimension=1, tiled=True)  180 us
    rev x1, local copies, waits for them, and re-layouts, diagonal_sums(): flipped = square[:, ::-1, :]  134 us
    reduce_scatter x6, waiting for transfers between devices, norm_backward(): lax.psum_scatter(grad_part, 'col', scatter_dimension=1, tiled=True)  127 us
  transfers between devices with their start and end apart: 40, of which 22 were waited for; matrix products, arithmetic and copies ran while one was open for 82% of the time, Pallas kernels for 0%

commit v1 on v0

--- a/solution.py
+++ b/solution.py
@@ -1,9 +1,15 @@
+import functools
+
 import jax
 import jax.numpy as jnp
 from jax import lax
+from jax.experimental import pallas as pl
+from jax.experimental.pallas import tpu as pltpu
 from jax.sharding import PartitionSpec as P
 
 NEG_FILL = -1000000000.0
+BLOCK = 256
+PAIR = 128
 
 
 def project(left, right):
@@ -26,60 +32,254 @@
     return jax.nn.gelu(values, approximate=True)
 
 
-def attention_scores(queries, key_rows, pos_bias, allowed):
-    scores = jnp.einsum("qhe,khe->hqk", queries, key_rows, preferred_element_type=jnp.float32)
-    if pos_bias is None:
-        return scores
-    return jnp.where(allowed[None], scores + pos_bias, NEG_FILL)
-
-
-def attend_forward(queries, key_rows, value_rows, pos_bias, allowed):
-    scores = attention_scores(queries, key_rows, pos_bias, allowed)
-    row_max = jnp.max(scores, axis=2, keepdims=True)
-    exp_scores = jnp.exp(scores - row_max)
-    row_total = jnp.sum(exp_scores, axis=2, keepdims=True)
-    attn_probs = (exp_scores / row_total).astype(jnp.bfloat16)
-    mixed = jnp.einsum("hqk,khe->qhe", attn_probs, value_rows, preferred_element_type=jnp.float32)
-    return (mixed.astype(jnp.bfloat16), row_max + jnp.log(row_total))
-
-
-def attend_backward(queries, key_rows, value_rows, pos_bias, allowed, log_total, grad_mixed):
-    scores = attention_scores(queries, key_rows, pos_bias, allowed)
-    attn_probs = jnp.exp(scores - log_total)
-    grad_values = jnp.einsum(
-        "hqk,qhe->khe",
-        attn_probs.astype(jnp.bfloat16),
-        grad_mixed,
-        preferred_element_type=jnp.float32,
-    )
-    grad_probs = jnp.einsum(
-        "qhe,khe->hqk", grad_mixed, value_rows, preferred_element_type=jnp.float32
-    )
-    grad_scores = attn_probs * (
-        grad_probs - jnp.sum(attn_probs * grad_probs, axis=2, keepdims=True)
-    )
-    grad_scores_low = grad_scores.astype(jnp.bfloat16)
-    grad_queries = jnp.einsum(
-        "hqk,khe->qhe", grad_scores_low, key_rows, preferred_element_type=jnp.float32
-    )
-    grad_keys = jnp.einsum(
-        "hqk,qhe->khe", grad_scores_low, queries, preferred_element_type=jnp.float32
-    )
-    return (
-        grad_queries.astype(jnp.bfloat16),
-        grad_keys.astype(jnp.bfloat16),
-        grad_values.astype(jnp.bfloat16),
-        grad_scores_low,
-    )
-
-
-def diagonal_sums(square):
-    head_count = square.shape[0]
-    length = square.shape[1]
-    flipped = square[:, ::-1, :]
-    padded = jnp.pad(flipped, ((0, 0), (0, 0), (0, length)))
-    flattened = padded.reshape(head_count, 2 * length * length)[:, : length * (2 * length - 1)]
-    return jnp.sum(flattened.reshape(head_count, length, 2 * length - 1), axis=1)
+def dot_nt(left, right):
+    return lax.dot_general(left, right, (((1,), (1,)), ((), ())), preferred_element_type=jnp.float32)
+
+
+def dot_nn(left, right):
+    return lax.dot_general(left, right, (((1,), (0,)), ((), ())), preferred_element_type=jnp.float32)
+
+
+def head_mask(head, head_size):
+    lane = lax.broadcasted_iota(jnp.int32, (1, PAIR), 1)
+    low = head * head_size
+    return ((lane >= low) & (lane < low + head_size)).astype(jnp.float32)
+
+
+def key_blocks(q_block, key_count, self_mode, prefix_blocks):
+    total = key_count // BLOCK
+    return min(total, max(q_block + 1, prefix_blocks)) if self_mode else total
+
+
+def forward_kernel(self_mode, q_count, key_count, key_valid, head_size, prefix_blocks, *refs):
+    if self_mode:
+        cut_ref, vec_ref, q_ref, k_ref, v_ref, o_ref, rest_ref, lse_ref, band = refs
+    else:
+        q_ref, k_ref, v_ref, o_ref, rest_ref, lse_ref = refs
+    head = pl.program_id(1)
+    mask = head_mask(head, head_size)
+    mask_low = mask.astype(jnp.bfloat16)
+    if self_mode:
+        wide = jnp.broadcast_to(vec_ref[0], (BLOCK, band.shape[1]))
+        band[...] = pltpu.roll(wide, 0, 1, stride=1, stride_axis=0)
+        cut = cut_ref[0]
+    base = q_count - BLOCK
+    col = lax.broadcasted_iota(jnp.int32, (BLOCK, BLOCK), 1)
+    row = lax.broadcasted_iota(jnp.int32, (BLOCK, BLOCK), 0)
+    for qb in range(q_count // BLOCK):
+        q_rows = pl.ds(qb * BLOCK, BLOCK)
+        query = q_ref[q_rows, :] * mask_low
+        parts = []
+        for kb in range(key_blocks(qb, key_count, self_mode, prefix_blocks)):
+            s = dot_nt(query, k_ref[pl.ds(kb * BLOCK, BLOCK), :])
+            if self_mode:
+                s = s + band[:, pl.ds((kb - qb) * BLOCK + base, BLOCK)]
+                if kb >= qb:
+                    limit = jnp.maximum(row + qb * BLOCK, cut - 1)
+                    s = jnp.where(col + kb * BLOCK <= limit, s, NEG_FILL)
+            elif (kb + 1) * BLOCK > key_valid:
+                s = jnp.where(col + kb * BLOCK < key_valid, s, NEG_FILL)
+            parts.append(s)
+        top = functools.reduce(jnp.maximum, [jnp.max(s, axis=1, keepdims=True) for s in parts])
+        total = jnp.zeros((BLOCK, 1), jnp.float32)
+        mixed = jnp.zeros((BLOCK, PAIR), jnp.float32)
+        for kb, s in enumerate(parts):
+            e = jnp.exp(s - top)
+            total = total + jnp.sum(e, axis=1, keepdims=True)
+            mixed = mixed + dot_nn(e.astype(jnp.bfloat16), v_ref[pl.ds(kb * BLOCK, BLOCK), :])
+        mixed = mixed * (mask / total)
+        mixed_low = mixed.astype(jnp.bfloat16)
+        rest = (mixed - mixed_low.astype(jnp.float32)).astype(jnp.bfloat16)
+
+        @pl.when(head == 0)
+        def _():
+            o_ref[q_rows, :] = mixed_low
+            rest_ref[q_rows, :] = rest
+
+        @pl.when(head > 0)
+        def _():
+            o_ref[q_rows, :] += mixed_low
+            rest_ref[q_rows, :] += rest
+
+        log_total = jnp.broadcast_to(top + jnp.log(total), (BLOCK, PAIR))
+        lse_ref[0, :, q_rows] = log_total.T[:1]
+
+
+def backward_kernel(self_mode, q_count, key_count, key_valid, head_size, prefix_blocks, *refs):
+    if self_mode:
+        cut_ref, vec_ref, q_ref, k_ref, v_ref, o_ref, rest_ref, do_ref, lse_ref = refs[:9]
+        dq_ref, dk_ref, dv_ref, diag_ref, kt, dqt, dk_acc, dv_acc, band, acc = refs[9:]
+    else:
+        q_ref, k_ref, v_ref, o_ref, rest_ref, do_ref, lse_ref = refs[:7]
+        dq_ref, dk_ref, dv_ref, kt, dqt, dk_acc, dv_acc = refs[7:]
+    head = pl.program_id(1)
+    mask = head_mask(head, head_size)
+    mask_low = mask.astype(jnp.bfloat16)
+    base = q_count - BLOCK
+
+    @pl.when(head == 0)
+    def _():
+        kt[...] = k_ref[...].T
+        dk_acc[...] = jnp.zeros_like(dk_acc)
+        dv_acc[...] = jnp.zeros_like(dv_acc)
+
+    if self_mode:
+        wide = jnp.broadcast_to(vec_ref[0], (BLOCK, band.shape[1]))
+        band[...] = pltpu.roll(wide, 0, 1, stride=1, stride_axis=0)
+        acc[...] = jnp.zeros_like(acc)
+        cut = cut_ref[0]
+    col = lax.broadcasted_iota(jnp.int32, (BLOCK, BLOCK), 1)
+    row = lax.broadcasted_iota(jnp.int32, (BLOCK, BLOCK), 0)
+    head_rows = pl.ds(pl.multiple_of(head * head_size, head_size), head_size)
+    key_t = kt[head_rows, :]
+    for qb in range(q_count // BLOCK):
+        q_rows = pl.ds(qb * BLOCK, BLOCK)
+        query = q_ref[q_rows, :] * mask_low
+        grad = do_ref[q_rows, :] * mask_low
+        mixed = o_ref[q_rows, :].astype(jnp.float32) + rest_ref[q_rows, :].astype(jnp.float32)
+        product = grad.astype(jnp.float32) * mixed
+        delta = jnp.sum(product.T, axis=0, keepdims=True)
+        log_total = lse_ref[0, :, q_rows]
+        dqt_sum = jnp.zeros((head_size, BLOCK), jnp.float32)
+        for kb in range(key_blocks(qb, key_count, self_mode, prefix_blocks)):
+            k_rows = pl.ds(kb * BLOCK, BLOCK)
+            s = dot_nt(k_ref[k_rows, :], query)
+            dp = dot_nt(v_ref[k_rows, :], grad)
+            if self_mode:
+                span = pl.ds((qb - kb) * BLOCK + base, BLOCK)
+                s = s + band[:, span]
+                if kb >= qb:
+                    limit = jnp.maximum(col + qb * BLOCK, cut - 1)
+                    s = jnp.where(row + kb * BLOCK <= limit, s, NEG_FILL)
+            elif (kb + 1) * BLOCK > key_valid:
+                s = jnp.where(row + kb * BLOCK < key_valid, s, NEG_FILL)
+            p = jnp.exp(s - log_total)
+            ds = p * (dp - delta)
+            ds_low = ds.astype(jnp.bfloat16)
+            if self_mode:
+                acc[:, span] += ds
+            dv_acc[k_rows, :] += dot_nn(p.astype(jnp.bfloat16), grad)
+            dk_acc[k_rows, :] += dot_nn(ds_low, query)
+            dqt_sum = dqt_sum + dot_nn(key_t[:, kb * BLOCK : (kb + 1) * BLOCK], ds_low)
+        dqt[head_rows, q_rows] = dqt_sum
+    if self_mode:
+        size = BLOCK
+        fold = acc[...]
+        lanes = fold.shape[1]
+        while size > 8:
+            size //= 2
+            fold = fold[:size] + pltpu.roll(fold[size:], lanes - size, 1)
+        diag_ref[0] = fold
+
+    @pl.when(head == pl.num_programs(1) - 1)
+    def _():
+        dq_ref[...] = dqt[...].T.astype(jnp.bfloat16)
+        dk_ref[...] = dk_acc[...].astype(jnp.bfloat16)
+        dv_ref[...] = dv_acc[...].astype(jnp.bfloat16)
+
+
+def lane_block(rows, offset):
+    return pl.BlockSpec((rows, PAIR), lambda p, h: (0, p + offset))
+
+
+def attention_forward(q_arr, k_arr, v_arr, offsets, head_count, head_size, key_valid, vec=None, cut=None, prefix_blocks=0):
+    q_count, key_count = q_arr.shape[0], k_arr.shape[0]
+    self_mode = vec is not None
+    per = PAIR // head_size
+    pairs = head_count // per
+    in_specs = [
+        lane_block(q_count, offsets[0]),
+        lane_block(key_count, offsets[1]),
+        lane_block(key_count, offsets[2]),
+    ]
+    args = [q_arr, k_arr, v_arr]
+    scratch = []
+    if self_mode:
+        lanes = vec.shape[-1]
+        in_specs = [
+            pl.BlockSpec(memory_space=pltpu.SMEM),
+            pl.BlockSpec((1, 1, lanes), lambda p, h: (p * per + h, 0, 0)),
+        ] + in_specs
+        args = [cut, vec] + args
+        scratch = [pltpu.VMEM((BLOCK, lanes), jnp.float32)]
+    return pl.pallas_call(
+        functools.partial(forward_kernel, self_mode, q_count, key_count, key_valid, head_size, prefix_blocks),
+        out_shape=(
+            jax.ShapeDtypeStruct((q_count, head_count * head_size), jnp.bfloat16),
+            jax.ShapeDtypeStruct((q_count, head_count * head_size), jnp.bfloat16),
+            jax.ShapeDtypeStruct((head_count, 1, q_count), jnp.float32),
+        ),
+        grid=(pairs, per),
+        in_specs=in_specs,
+        out_specs=(
+            lane_block(q_count, 0),
+            lane_block(q_count, 0),
+            pl.BlockSpec((1, 1, q_count), lambda p, h: (p * per + h, 0, 0)),
+        ),
+        scratch_shapes=scratch,
+        compiler_params=pltpu.CompilerParams(vmem_limit_bytes=40 << 20),
+        cost_estimate=pl.CostEstimate(
+            flops=4 * head_count * q_count * key_count * PAIR,
+            bytes_accessed=4 * head_count * q_count * head_size * 2,
+            transcendentals=head_count * q_count * key_count,
+        ),
+        name="self_forward" if self_mode else "cross_forward",
+    )(*args)
+
+
+def attention_backward(q_arr, k_arr, v_arr, offsets, out, rest, grad, log_total, head_count, head_size, key_valid, vec=None, cut=None, prefix_blocks=0):
+    q_count, key_count = q_arr.shape[0], k_arr.shape[0]
+    self_mode = vec is not None
+    per = PAIR // head_size
+    pairs = head_count // per
+    width = head_count * head_size
+    in_specs = [
+        lane_block(q_count, offsets[0]),
+        lane_block(key_count, offsets[1]),
+        lane_block(key_count, offsets[2]),
+        lane_block(q_count, 0),
+        lane_block(q_count, 0),
+        lane_block(q_count, 0),
+        pl.BlockSpec((1, 1, q_count), lambda p, h: (p * per + h, 0, 0)),
+    ]
+    args = [q_arr, k_arr, v_arr, out, rest, grad, log_total]
+    scratch = [
+        pltpu.VMEM((PAIR, key_count), jnp.bfloat16),
+        pltpu.VMEM((PAIR, q_count), jnp.float32),
+        pltpu.VMEM((key_count, PAIR), jnp.float32),
+        pltpu.VMEM((key_count, PAIR), jnp.float32),
+    ]
+    out_shape = [
+        jax.ShapeDtypeStruct((q_count, width), jnp.bfloat16),
+        jax.ShapeDtypeStruct((key_count, width), jnp.bfloat16),
+        jax.ShapeDtypeStruct((key_count, width), jnp.bfloat16),
+    ]
+    out_specs = [lane_block(q_count, 0), lane_block(key_count, 0), lane_block(key_count, 0)]
+    if self_mode:
+        lanes = vec.shape[-1]
+        in_specs = [
+            pl.BlockSpec(memory_space=pltpu.SMEM),
+            pl.BlockSpec((1, 1, lanes), lambda p, h: (p * per + h, 0, 0)),
+        ] + in_specs
+        args = [cut, vec] + args
+        scratch += [pltpu.VMEM((BLOCK, lanes), jnp.float32), pltpu.VMEM((BLOCK, lanes), jnp.float32)]
+        out_shape.append(jax.ShapeDtypeStruct((head_count, 8, lanes), jnp.float32))
+        out_specs.append(pl.BlockSpec((1, 8, lanes), lambda p, h: (p * per + h, 0, 0)))
+    return pl.pallas_call(
+        functools.partial(backward_kernel, self_mode, q_count, key_count, key_valid, head_size, prefix_blocks),
+        out_shape=tuple(out_shape),
+        grid=(pairs, per),
+        in_specs=in_specs,
+        out_specs=tuple(out_specs),
+        scratch_shapes=scratch,
+        compiler_params=pltpu.CompilerParams(vmem_limit_bytes=40 << 20),
+        cost_estimate=pl.CostEstimate(
+            flops=10 * head_count * q_count * key_count * PAIR,
+            bytes_accessed=8 * head_count * q_count * head_size * 2,
+            transcendentals=head_count * q_count * key_count,
+        ),
+        name="self_backward" if self_mode else "cross_backward",
+    )(*args)
 
 
 def normalize(resid_rows, gain_vec):
@@ -94,7 +294,9 @@
 
 def norm_backward(grad_part, resid_rows, inv_scale, gain_vec):
     model_width = resid_rows.shape[1] * lax.axis_size("col")
-    grad_normed = lax.psum_scatter(grad_part, "col", scatter_dimension=1, tiled=True)
+    grad_normed = lax.psum_scatter(
+        grad_part.astype(jnp.bfloat16), "col", scatter_dimension=1, tiled=True
+    ).astype(jnp.float32)
     scaled = grad_normed * gain_vec
     inner_sum = lax.psum(jnp.sum(scaled * resid_rows, axis=1), "col")
     grad_resid = (
@@ -106,7 +308,9 @@
 
 
 def branch_sum(partial_rows):
-    return lax.psum_scatter(partial_rows, "col", scatter_dimension=1, tiled=True)
+    return lax.psum_scatter(
+        partial_rows.astype(jnp.bfloat16), "col", scatter_dimension=1, tiled=True
+    ).astype(jnp.float32)
 
 
 def branch_grad(grad_rows):
@@ -177,13 +381,13 @@
     distance_bias = jnp.dot(
         bucket_onehot, full_bias.astype(jnp.float32), precision=lax.Precision.HIGHEST
     ).T
-    places = jnp.arange(seq_len, dtype=jnp.int32)
-    offsets = places[None, :] - places[:, None] + seq_len - 1
-    pos_bias = jnp.take(distance_bias, offsets, axis=1)
-    causal = places[None, :] <= places[:, None]
-
-    def split_heads(flat_rows, count):
-        return flat_rows.reshape(seq_count, count, head_count, head_size)
+    def band_rows(vector):
+        return jnp.roll(jnp.pad(vector, ((0, 0), (0, 1))), 1 - BLOCK, axis=1)[:, None, :]
+
+    band_forward = band_rows(distance_bias)
+    band_backward = band_rows(distance_bias[:, ::-1])
+    prefix_blocks = -(-(seq_len // 2) // BLOCK)
+    pairs = head_count * head_size // PAIR
 
     outputs = []
     grad_inputs = []
@@ -196,48 +400,30 @@
         jnp.zeros((inner_width, model_width), jnp.float32),
         jnp.zeros((model_width, ffn_width), jnp.float32),
         jnp.zeros((ffn_width, model_width), jnp.float32),
-        jnp.zeros((head_count, seq_len, seq_len), jnp.float32),
+        jnp.zeros((head_count, 8, 2 * seq_len), jnp.float32),
     ]
     gain_sums = [jnp.zeros(norm_self.shape, jnp.float32) for _ in range(3)]
     for micro_step in range(micro_count):
         resid_zero = residual_in[micro_step]
         normed_one, scale_one = normalize(resid_zero, norm_self)
-        qkv_rows = (
-            project(normed_one, qkv_weight)
-            .astype(low_type)
-            .reshape(seq_count, seq_len, 3, head_count, head_size)
-        )
-        queries, key_rows, value_rows = (qkv_rows[:, :, 0], qkv_rows[:, :, 1], qkv_rows[:, :, 2])
-
-        def self_forward(pieces):
-            query_seq, key_seq, value_seq, cut_len = pieces
-            allowed = causal | (places[None, :] < cut_len)
-            return attend_forward(query_seq, key_seq, value_seq, pos_bias, allowed)
-
-        self_mix, self_total = lax.map(
-            self_forward, (queries, key_rows, value_rows, prefix_len[micro_step])
-        )
-        self_flat = self_mix.reshape(token_rows, inner_width)
+        qkv_rows = project(normed_one, qkv_weight).astype(low_type)
+        cut_len = prefix_len[micro_step]
+        self_flat, self_rest, self_total = attention_forward(
+            qkv_rows, qkv_rows, qkv_rows, (0, pairs, 2 * pairs), head_count, head_size, seq_len,
+            band_forward, cut_len, prefix_blocks,
+        )
         resid_one = resid_zero + branch_sum(project(self_flat, full_self_out))
         normed_two, scale_two = normalize(resid_one, norm_cross)
-        cross_queries = split_heads(project(normed_two, full_cross_query).astype(low_type), seq_len)
+        cross_queries = project(normed_two, full_cross_query).astype(low_type)
         memory_rows = lax.all_gather(
             encoder_out[micro_step].astype(low_type), "col", axis=1, tiled=True
         )
-        memory_len = memory_rows.shape[0] // seq_count
-        kv_rows = (
-            project(memory_rows, kv_weight)
-            .astype(low_type)
-            .reshape(seq_count, memory_len, 2, head_count, head_size)
-        )
-        cross_keys, cross_values = (kv_rows[:, :, 0], kv_rows[:, :, 1])
-
-        def cross_forward(pieces):
-            query_seq, key_seq, value_seq = pieces
-            return attend_forward(query_seq, key_seq, value_seq, None, None)
-
-        cross_mix, cross_total = lax.map(cross_forward, (cross_queries, cross_keys, cross_values))
-        cross_flat = cross_mix.reshape(token_rows, inner_width)
+        memory_len = memory_rows.shape[0]
+        memory_rows = jnp.pad(memory_rows, ((0, -memory_len % BLOCK), (0, 0)))
+        kv_rows = project(memory_rows, kv_weight).astype(low_type)
+        cross_flat, cross_rest, cross_total = attention_forward(
+            cross_queries, kv_rows, kv_rows, (0, 0, pairs), head_count, head_size, memory_len
+        )
         resid_two = resid_one + branch_sum(project(cross_flat, full_cross_out))
         normed_three, scale_three = normalize(resid_two, norm_ffn)
         ffn_pre = project(normed_three, full_ffn_in)
@@ -256,29 +442,17 @@
         grad_two = grad_two + grad_top
         grad_rows = branch_grad(grad_two)
         running[4] = running[4] + project_left(cross_flat, grad_rows)
-        grad_cross_mix = split_heads(
-            project_back(grad_rows, full_cross_out).astype(low_type), seq_len
-        )
-
-        def cross_backward(pieces):
-            query_seq, key_seq, value_seq, total_seq, grad_seq = pieces
-            grad_query, grad_key, grad_value, grad_scores_low = attend_backward(
-                query_seq, key_seq, value_seq, None, None, total_seq, grad_seq
-            )
-            return (grad_query, grad_key, grad_value)
-
-        cross_grad_query, cross_grad_key, cross_grad_value = lax.map(
-            cross_backward, (cross_queries, cross_keys, cross_values, cross_total, grad_cross_mix)
-        )
-        cross_grad_flat = cross_grad_query.reshape(token_rows, inner_width)
-        grad_kv = jnp.stack((cross_grad_key, cross_grad_value), axis=2).reshape(
-            seq_count * memory_len, 2 * inner_width
-        )
+        grad_cross_mix = project_back(grad_rows, full_cross_out).astype(low_type)
+        cross_grad_flat, cross_grad_key, cross_grad_value = attention_backward(
+            cross_queries, kv_rows, kv_rows, (0, 0, pairs), cross_flat, cross_rest, grad_cross_mix, cross_total,
+            head_count, head_size, memory_len,
+        )
+        grad_kv = jnp.concatenate((cross_grad_key, cross_grad_value), axis=1)
         running[2] = running[2] + project_left(normed_two, cross_grad_flat)
         running[3] = running[3] + project_left(memory_rows, grad_kv)
         grad_memory.append(
             lax.psum_scatter(
-                project_back(grad_kv, kv_weight).astype(jnp.bfloat16),
+                project_back(grad_kv, kv_weight)[:memory_len].astype(jnp.bfloat16),
                 "col",
                 scatter_dimension=1,
                 tiled=True,
@@ -291,39 +465,24 @@
         grad_one = grad_one + grad_two
         grad_rows = branch_grad(grad_one)
         running[1] = running[1] + project_left(self_flat, grad_rows)
-        grad_self_mix = split_heads(
-            project_back(grad_rows, full_self_out).astype(low_type), seq_len
-        )
-
-        def self_backward(square_sum, pieces):
-            query_seq, key_seq, value_seq, cut_len, total_seq, grad_seq = pieces
-            allowed = causal | (places[None, :] < cut_len)
-            grad_query, grad_key, grad_value, grad_scores_low = attend_backward(
-                query_seq, key_seq, value_seq, pos_bias, allowed, total_seq, grad_seq
-            )
-            return (
-                square_sum + grad_scores_low.astype(jnp.float32),
-                (grad_query, grad_key, grad_value),
-            )
-
-        bias_square, (self_grad_query, self_grad_key, self_grad_value) = lax.scan(
-            self_backward,
-            running[7],
-            (queries, key_rows, value_rows, prefix_len[micro_step], self_total, grad_self_mix),
-        )
-        running[7] = bias_square
-        grad_qkv = jnp.stack((self_grad_query, self_grad_key, self_grad_value), axis=2).reshape(
-            token_rows, 3 * inner_width
-        )
+        grad_self_mix = project_back(grad_rows, full_self_out).astype(low_type)
+        self_grad_query, self_grad_key, self_grad_value, diag_part = attention_backward(
+            qkv_rows, qkv_rows, qkv_rows, (0, pairs, 2 * pairs), self_flat, self_rest, grad_self_mix, self_total,
+            head_count, head_size, seq_len, band_backward, cut_len, prefix_blocks,
+        )
+        running[7] = running[7] + diag_part
+        grad_qkv = jnp.concatenate((self_grad_query, self_grad_key, self_grad_value), axis=1)
         running[0] = running[0] + project_left(normed_one, grad_qkv)
         grad_zero, gain_part = norm_backward(
             project_back(grad_qkv, qkv_weight), resid_zero, scale_one, norm_self
         )
         gain_sums[0] = gain_sums[0] + gain_part
         grad_inputs.append(grad_zero + grad_one)
-    bias_grad = jnp.dot(
-        bucket_onehot.T, diagonal_sums(running[7]).T, precision=lax.Precision.HIGHEST
-    )
+    diagonals = sum(jnp.roll(running[7][:, row], -row, axis=1) for row in range(8))
+    place_onehot = jnp.roll(
+        jnp.pad(bucket_onehot[::-1], ((0, 1), (0, 0))), 1 - BLOCK, axis=0
+    )
+    bias_grad = jnp.dot(place_onehot.T, diagonals.T, precision=lax.Precision.HIGHEST)
     weight_grads = (
         lax.psum_scatter(
             running[0][:, :inner_width].astype(jnp.bfloat16),

time: 6080 us -> 1660 us (0.27); the launches traced: 5990 us -> 1650 us
  local copies, waits for them, and re-layouts: 4480 us -> 50.1 us
  waiting for transfers between devices: 748 us -> 1050 us
  matrix products: 358 us -> 144 us
  other arithmetic: 168 us -> 57.1 us
  Pallas kernels: 0 us -> 110 us
    gather x2 -> x0, local copies, waits for them, and re-layouts: 4050 us -> none  [body(): pos_bias = jnp.take(distance_bias, offsets, axis=1)]
    dot_general x25 -> x1, matrix products: 193 us -> 0.39 us  [body(): jnp.dot(place_onehot.T, diagonals.T, precision=lax.Precision.HIGHEST)]
    unnamed x268 -> x218, local copies, waits for them, and re-layouts: 205 us -> 36.3 us
    rev x1 -> x0, local copies, waits for them, and re-layouts: 134 us -> none  [diagonal_sums(): flipped = square[:, ::-1, :]]
    reduce_scatter x14 -> x16, waiting for transfers between devices: 373 us -> 486 us  [the longest x6 153 us: norm_backward(): lax.psum_scatter(grad_part.astype(jnp.bfloat16), 'col', scatter_dimension...]
    pallas_call x0 -> x8, Pallas kernels: none -> 110 us  [the longest x4 63.9 us: attention_backward(): pl.pallas_call(functools.partial(backward_kernel, self_mode, q_count, key...]
    unnamed x45 -> x43, waiting for transfers between devices: 180 us -> 105 us
    reduce_scatter x1, waiting for transfers between devices: 0.01 us -> 67.4 us  [body(): lax.psum_scatter(running[5].astype(jnp.bfloat16), ('dp', 'row'), scatter_...]
  transfers between devices with their start and end apart: 40 -> 40, of which waited for: 22 -> 29; matrix products, arithmetic and copies ran while one was open for 82% -> 11% of each run, Pallas kernels for 0% -> 7%
where the time goes in v1:
time: 1660 us; the launch traced here: 1650 us
  waiting for transfers between devices  1050 us (63%)
  blocking collectives  219 us (13%)
  matrix products  144 us (9%)
  Pallas kernels  110 us (7%)
  other arithmetic  57.1 us (3%)
  local copies, waits for them, and re-layouts  50.1 us (3%)
  between operations  18.6 us (1%)
    reduce_scatter x6, waiting for transfers between devices, norm_backward(): lax.psum_scatter(grad_part.astype(jnp.bfloat16), 'col', scatter_dimension...  153 us
    reduce_scatter x6, waiting for transfers between devices, branch_sum(): lax.psum_scatter(partial_rows.astype(jnp.bfloat16), 'col', scatter_dimens...  141 us
    unnamed x43, waiting for transfers between devices  105 us
    reduce_scatter x1, waiting for transfers between devices, body(): lax.psum_scatter(running[5].astype(jnp.bfloat16), ('dp', 'row'), scatter_...  67.4 us
    reduce_scatter x2, waiting for transfers between devices, body(): lax.psum_scatter(project_back(grad_kv, kv_weight)[:memory_len].astype(jnp...  65.5 us
    pallas_call x4, Pallas kernels, attention_backward(): pl.pallas_call(functools.partial(backward_kernel, self_mode, q_count, key...  63.9 us
    reduce_scatter x1, waiting for transfers between devices, body(): lax.psum_scatter(running[2].astype(jnp.bfloat16), ('dp', 'row'), scatter_...  63.2 us
    reduce_scatter x1, waiting for transfers between devices, body(): lax.psum_scatter(running[3][:, inner_width:].astype(jnp.bfloat16), ('dp',...  63.1 us
  transfers between devices with their start and end apart: 40, of which 29 were waited for; matrix products, arithmetic and copies ran while one was open for 11% of the time, Pallas kernels for 7%

profile of v1, /device:TPU:0, one launch (start us, length us, event | category | flops | bytes accessed | tf_op | source)
XLA Modules:
  0.0 1650.8 jit_solution(9418477127346433878)
XLA Ops:
  21.0 11.2 all-gather.2
  34.0 14.8 all_gather.77
  48.8 15.9 all_gather.78
  64.8 16.1 all_gather.79
  80.9 14.7 all_gather.80
  99.1 11.5 self_forward.2
  117.8 11.5 self_forward.3
  144.4 34.6 %reduce-scatter.37.cloned.1.call-done = bf16[1024,256]{1,0:T(8,128)(2,1)} async-done(((bf16[1024,1024]{1,0:T(8,128)(2,1)}), bf16[1024,256]{1,0:T(8,128)(2,1)}) %reduce-scatter.37.cloned.1.call-update) | async-done | bytes 524304 | tf_op jit(solution)/shard_map/reduce_scatter | solution.py:311
  190.2 15.7 all_gather.84
  205.9 17.3 %all_gather.85 = bf16[1024,256]{1,0:T(8,128)(2,1)S(1)} all-gather(bf16[256,256]{1,0:T(8,128)(2,1)S(1)} %convert_element_type.277), channel_id=1, replica_groups=mesh['dp'=2,'row'=4,'col'=4] {'row'}, dimensions={0}, use_global_device_ids=true | all-gather | bytes 655360 | tf_op jit(solution)/shard_map/all_gather | solution.py:356
  223.3 16.3 all_gather.86
  239.6 15.2 all_gather.82
  260.6 11.3 cross_forward.3
  279.8 11.3 cross_forward.2
  300.4 11.2 reduce-scatter.39.cloned.1.call-done
  312.8 33.3 %reduce-scatter.33.cloned.1.call-done = bf16[1024,256]{1,0:T(8,128)(2,1)} async-done(((bf16[1024,1024]{1,0:T(8,128)(2,1)}), bf16[1024,256]{1,0:T(8,128)(2,1)}) %reduce-scatter.33.cloned.1.call-update) | async-done | bytes 524304 | tf_op jit(solution)/shard_map/reduce_scatter | solution.py:311
  356.2 9.9 all-gather.36.cloned.1.call-done
  372.6 40.4 %all-gather.26.cloned.1.call-done = bf16[1024,1024]{1,0:T(8,128)(2,1)} async-done(((bf16[256,1024]{1,0:T(8,128)(2,1)}), bf16[1024,1024]{1,0:T(8,128)(2,1)}) %all-gather.26.cloned.1.call-update) | async-done | bytes 2097168 | tf_op jit(solution)/shard_map/all_gather | solution.py:358
  413.1 23.7 %all-gather.24.cloned.1.call-done = bf16[1024,1024]{1,0:T(8,128)(2,1)} async-done(((bf16[1024,256]{1,0:T(8,128)(2,1)}), bf16[1024,1024]{1,0:T(8,128)(2,1)}) %all-gather.24.cloned.1.call-update) | async-done | bytes 2097168 | tf_op jit(solution)/shard_map/all_gather | solution.py:289
  436.7 10.0 fusion.6
  452.6 30.7 %reduce-scatter.43.cloned.1.call-done = bf16[1024,256]{1,0:T(8,128)(2,1)} async-done(((bf16[1024,1024]{1,0:T(8,128)(2,1)}), bf16[1024,256]{1,0:T(8,128)(2,1)}) %reduce-scatter.43.cloned.1.call-update) | async-done | bytes 524304 | tf_op jit(solution)/shard_map/reduce_scatter | solution.py:297
  486.5 21.7 %all-gather.42.cloned.1.call-done = bf16[1024,1024]{1,0:T(8,128)(2,1)} async-done(((bf16[1024,256]{1,0:T(8,128)(2,1)}), bf16[1024,1024]{1,0:T(8,128)(2,1)}) %all-gather.42.cloned.1.call-update) | async-done | bytes 2097168 | tf_op jit(solution)/shard_map/all_gather | solution.py:317
  514.8 18.2 %all-gather.34.cloned.1.call-done = bf16[1024,1024]{1,0:T(8,128)(2,1)} async-done(((bf16[1024,256]{1,0:T(8,128)(2,1)}), bf16[1024,1024]{1,0:T(8,128)(2,1)}) %all-gather.34.cloned.1.call-update) | async-done | bytes 2097168 | tf_op jit(solution)/shard_map/all_gather | solution.py:289
  533.0 10.0 fusion.13
  555.0 24.5 %reduce-scatter.49.cloned.1.call-done = bf16[1024,256]{1,0:T(8,128)(2,1)} async-done(((bf16[1024,1024]{1,0:T(8,128)(2,1)}), bf16[1024,256]{1,0:T(8,128)(2,1)}) %reduce-scatter.49.cloned.1.call-update) | async-done | bytes 524304 | tf_op jit(solution)/shard_map/reduce_scatter | solution.py:297
  587.1 26.8 %reduce-scatter.41.cloned.1.call-done = bf16[1024,256]{1,0:T(8,128)(2,1)} async-done(((bf16[1024,1024]{1,0:T(8,128)(2,1)}), bf16[1024,256]{1,0:T(8,128)(2,1)}) %reduce-scatter.41.cloned.1.call-update) | async-done | bytes 524304 | tf_op jit(solution)/shard_map/reduce_scatter | solution.py:311
  618.8 21.9 %all-gather.44.cloned.1.call-done = bf16[1024,1024]{1,0:T(8,128)(2,1)} async-done(((bf16[1024,256]{1,0:T(8,128)(2,1)}), bf16[1024,1024]{1,0:T(8,128)(2,1)}) %all-gather.44.cloned.1.call-update) | async-done | bytes 2097168 | tf_op jit(solution)/shard_map/all_gather | solution.py:317
  644.4 16.5 %cross_backward.3 = (bf16[1024,256]{1,0:T(8,128)(2,1)S(1)}, bf16[1024,256]{1,0:T(8,128)(2,1)S(1)}, bf16[1024,256]{1,0:T(8,128)(2,1)S(1)}) custom-call(bf16[1024,256]{1,0:T(8,128)(2,1)S(1)} %convolution_convert_fusion.18.refs_0_, bf16[1024,512]{1,0:T(8,128)(2,1)S(1)} %copy-done.21, bf16[1024,512]{1,0:T(8,128)(2,1)S(1)} %copy-done.21, ...), custom_call_target="tpu_custom_call" | custom-call | flops 5368709120 | bytes 4194304 | tf_op jit(solution)/shard_map/cross_backward/pallas_call | solution.py:268
  671.2 16.5 %cross_backward.2 = (bf16[1024,256]{1,0:T(8,128)(2,1)S(1)}, bf16[1024,256]{1,0:T(8,128)(2,1)S(1)}, bf16[1024,256]{1,0:T(8,128)(2,1)S(1)}) custom-call(bf16[1024,256]{1,0:T(8,128)(2,1)S(1)} %copy-done.9, bf16[1024,512]{1,0:T(8,128)(2,1)S(1)} %copy-done.19, bf16[1024,512]{1,0:T(8,128)(2,1)S(1)} %copy-done.19, bf16[1024,256]{1,0:T(8,128)(2,1)S(1)} %get-tuple-element.44.refs_3_, ...), custom_call_target="tpu_custom_call" | custom-call | flops 5368709120 | bytes 4194304 | tf_op jit(solution)/shard_map/cross_backward/pallas_call | solution.py:268
  698.1 31.8 %reduce-scatter.45.cloned.1.call-done = bf16[1024,256]{1,0:T(8,128)(2,1)} async-done(((bf16[1024,1024]{1,0:T(8,128)(2,1)}), bf16[1024,256]{1,0:T(8,128)(2,1)}) %reduce-scatter.45.cloned.1.call-update) | async-done | bytes 524304 | tf_op jit(solution)/shard_map/reduce_scatter | solution.py:297
  738.4 25.6 %reduce-scatter.35.cloned.1.call-done = bf16[1024,256]{1,0:T(8,128)(2,1)} async-done(((bf16[1024,1024]{1,0:T(8,128)(2,1)}), bf16[1024,256]{1,0:T(8,128)(2,1)}) %reduce-scatter.35.cloned.1.call-update) | async-done | bytes 524304 | tf_op jit(solution)/shard_map/reduce_scatter | solution.py:311
  828.4 15.5 self_backward.2
  846.3 15.4 self_backward.3
  890.6 67.4 %reduce-scatter.71.cloned.1.call-done = bf16[128,1024]{1,0:T(8,128)(2,1)} async-done(((bf16[1024,1024]{1,0:T(8,128)(2,1)}), bf16[128,1024]{1,0:T(8,128)(2,1)}) %reduce-scatter.71.cloned.1.call-update) | async-done | bytes 262160 | tf_op jit(solution)/shard_map/reduce_scatter | solution.py:526
  959.8 62.5 %reduce-scatter.75.cloned.1.call-done = bf16[128,256]{1,0:T(8,128)(2,1)} async-done(((bf16[1024,256]{1,0:T(8,128)(2,1)}), bf16[128,256]{1,0:T(8,128)(2,1)}) %reduce-scatter.75.cloned.1.call-update) | async-done | bytes 65552
  1023.9 63.2 %reduce-scatter.65.cloned.1.call-done = bf16[128,256]{1,0:T(8,128)(2,1)} async-done(((bf16[1024,256]{1,0:T(8,128)(2,1)}), bf16[128,256]{1,0:T(8,128)(2,1)}) %reduce-scatter.65.cloned.1.call-update) | async-done | bytes 65552 | tf_op jit(solution)/shard_map/reduce_scatter | solution.py:508
  1088.6 62.9 %reduce-scatter.67.cloned.1.call-done = bf16[128,256]{1,0:T(8,128)(2,1)} async-done(((bf16[1024,256]{1,0:T(8,128)(2,1)}), bf16[128,256]{1,0:T(8,128)(2,1)}) %reduce-scatter.67.cloned.1.call-update) | async-done | bytes 65552 | tf_op jit(solution)/shard_map/reduce_scatter | solution.py:511
  1153.0 63.1 %reduce-scatter.69.cloned.1.call-done = bf16[128,256]{1,0:T(8,128)(2,1)} async-done(((bf16[1024,256]{1,0:T(8,128)(2,1)}), bf16[128,256]{1,0:T(8,128)(2,1)}) %reduce-scatter.69.cloned.1.call-update) | async-done | bytes 65552 | tf_op jit(solution)/shard_map/reduce_scatter | solution.py:517
  1217.6 31.8 %reduce-scatter.57.cloned.1.call-done = bf16[1000,256]{1,0:T(8,128)(2,1)} async-done(((bf16[1000,1024]{1,0:T(8,128)(2,1)}), bf16[1000,256]{1,0:T(8,128)(2,1)}) %reduce-scatter.57.cloned.1.call-update) | async-done | bytes 512016 | tf_op jit(solution)/shard_map/reduce_scatter | solution.py:454
  1249.4 33.7 %reduce-scatter.55.cloned.1.call-done = bf16[1000,256]{1,0:T(8,128)(2,1)} async-done(((bf16[1000,1024]{1,0:T(8,128)(2,1)}), bf16[1000,256]{1,0:T(8,128)(2,1)}) %reduce-scatter.55.cloned.1.call-update) | async-done | bytes 512016 | tf_op jit(solution)/shard_map/reduce_scatter | solution.py:454
  1288.6 21.9 %all-reduce.5 = bf16[32,4]{1,0:T(8,128)(2,1)S(1)} all-reduce(bf16[32,4]{1,0:T(8,128)(2,1)S(1)} %convolution_convert_fusion.20), channel_id=28, replica_groups=mesh['dp'=2,'row'=4,'col'=4] {'dp','row'}, use_global_device_ids=true, to_apply=%region_57.58.clone | all-reduce | flops 128 | bytes 512
  1311.1 37.2 %reduce-scatter.73.cloned.1.call-done = bf16[128,256]{1,0:T(8,128)(2,1)} async-done(((bf16[1024,256]{1,0:T(8,128)(2,1)}), bf16[128,256]{1,0:T(8,128)(2,1)}) %reduce-scatter.73.cloned.1.call-update) | async-done | bytes 65552
  1349.9 63.0 %reduce-scatter.59.cloned.1.call-done = bf16[128,256]{1,0:T(8,128)(2,1)} async-done(((bf16[1024,256]{1,0:T(8,128)(2,1)}), bf16[128,256]{1,0:T(8,128)(2,1)}) %reduce-scatter.59.cloned.1.call-update) | async-done | bytes 65552 | tf_op jit(solution)/shard_map/reduce_scatter | solution.py:487
  1414.4 62.9 %reduce-scatter.61.cloned.1.call-done = bf16[128,256]{1,0:T(8,128)(2,1)} async-done(((bf16[1024,256]{1,0:T(8,128)(2,1)}), bf16[128,256]{1,0:T(8,128)(2,1)}) %reduce-scatter.61.cloned.1.call-update) | async-done | bytes 65552 | tf_op jit(solution)/shard_map/reduce_scatter | solution.py:493
  1478.8 63.1 %reduce-scatter.63.cloned.1.call-done = bf16[128,256]{1,0:T(8,128)(2,1)} async-done(((bf16[1024,256]{1,0:T(8,128)(2,1)}), bf16[128,256]{1,0:T(8,128)(2,1)}) %reduce-scatter.63.cloned.1.call-update) | async-done | bytes 65552 | tf_op jit(solution)/shard_map/reduce_scatter | solution.py:499
  1543.4 32.0 %reduce-scatter.47.cloned.1.call-done = bf16[1024,256]{1,0:T(8,128)(2,1)} async-done(((bf16[1024,1024]{1,0:T(8,128)(2,1)}), bf16[1024,256]{1,0:T(8,128)(2,1)}) %reduce-scatter.47.cloned.1.call-update) | async-done | bytes 524304 | tf_op jit(solution)/shard_map/reduce_scatter | solution.py:297
  1575.4 34.1 %reduce-scatter.53.cloned.1.call-done = bf16[1024,256]{1,0:T(8,128)(2,1)} async-done(((bf16[1024,1024]{1,0:T(8,128)(2,1)}), bf16[1024,256]{1,0:T(8,128)(2,1)}) %reduce-scatter.53.cloned.1.call-update) | async-done | bytes 524304 | tf_op jit(solution)/shard_map/reduce_scatter | solution.py:297
  1621.0 22.2 %all-reduce.6 = (f32[256]{0:T(256)}, f32[256]{0:T(256)}, f32[256]{0:T(256)}) all-reduce(f32[256]{0:T(256)S(1)} %add.234, f32[256]{0:T(256)S(1)} %add.235, f32[256]{0:T(256)S(1)} %add.236), channel_id=1, replica_groups=mesh['dp'=2,'row'=4,'col'=4] {'dp','row'}, use_global_device_ids=true, to_apply=%region_40.41 | all-reduce | flops 768 | bytes 6144 | tf_op jit(solution)/shard_map/psum | solution.py:536
  (457 shorter events, 290.3 us)
Async XLA Ops:
  8.0 87.5 %all-gather.20.cloned.1.call-start = ((), (), s32[]{:S(2)}) async-start(), calls=%async_computation.24 | async-start | bytes 2621440 | tf_op jit(solution)/shard_map/all_gather | solution.py:289
  20.2 94.2 %all-gather.30.cloned.1.call-start = ((), (), s32[]{:S(2)}) async-start(), calls=%async_computation.32 | async-start | bytes 2621440 | tf_op jit(solution)/shard_map/all_gather | solution.py:289
  21.0 123.4 %reduce-scatter.31.cloned.1.call-start = ((), (), s32[]{:S(2)}) async-start(), calls=%async_computation.25 | async-start | bytes 2621440 | tf_op jit(solution)/shard_map/reduce_scatter | solution.py:311
  114.4 64.6 %reduce-scatter.37.cloned.1.call-start = ((), (), s32[]{:S(2)}) async-start(), calls=%async_computation.33 | async-start | bytes 2621440 | tf_op jit(solution)/shard_map/reduce_scatter | solution.py:311
  133.0 121.8 %all-gather.50.cloned.1.call-start = ((), (), s32[]{:S(2)}) async-start(), calls=%async_computation.60 | async-start | bytes 2560000 | tf_op jit(solution)/shard_map/all_gather | solution.py:418
  134.3 123.6 %all-gather.32.cloned.1.call-start = ((), (), s32[]{:S(2)}) async-start(), calls=%async_computation.34 | async-start | bytes 2621440 | tf_op jit(solution)/shard_map/all_gather | solution.py:289
  188.5 85.5 %all-gather.48.cloned.1.call-start = ((), (), s32[]{:S(2)}) async-start(), calls=%async_computation.59 | async-start | bytes 2560000 | tf_op jit(solution)/shard_map/all_gather | solution.py:418
  189.2 87.9 %all-gather.22.cloned.1.call-start = ((), (), s32[]{:S(2)}) async-start(), calls=%async_computation.26 | async-start | bytes 2621440 | tf_op jit(solution)/shard_map/all_gather | solution.py:289
  190.0 121.6 %reduce-scatter.39.cloned.1.call-start = ((), (), s32[]{:S(2)}) async-start(), calls=%async_computation.35 | async-start | bytes 2621440 | tf_op jit(solution)/shard_map/reduce_scatter | solution.py:311
  273.9 72.2 %reduce-scatter.33.cloned.1.call-start = ((), (), s32[]{:S(2)}) async-start(), calls=%async_computation.27 | async-start | bytes 2621440 | tf_op jit(solution)/shard_map/reduce_scatter | solution.py:311
  294.0 62.2 %all-gather.28.cloned.1.call-start = ((), (), s32[]{:S(2)}) async-start(), calls=%async_computation.30 | async-start | bytes 2621440 | tf_op jit(solution)/shard_map/all_gather | solution.py:359
  294.9 71.1 %all-gather.36.cloned.1.call-start = ((), (), s32[]{:S(2)}) async-start(), calls=%async_computation.38 | async-start | bytes 2621440 | tf_op jit(solution)/shard_map/all_gather | solution.py:317
  297.7 115.3 %all-gather.26.cloned.1.call-start = ((), (), s32[]{:S(2)}) async-start(), calls=%async_computation.29 | async-start | bytes 2621440 | tf_op jit(solution)/shard_map/all_gather | solution.py:358
  299.9 136.8 %all-gather.24.cloned.1.call-start = ((), (), s32[]{:S(2)}) async-start(), calls=%async_computation.28 | async-start | bytes 2621440 | tf_op jit(solution)/shard_map/all_gather | solution.py:289
  356.1 127.2 %reduce-scatter.43.cloned.1.call-start = ((), (), s32[]{:S(2)}) async-start(), calls=%async_computation.39 | async-start | bytes 2621440 | tf_op jit(solution)/shard_map/reduce_scatter | solution.py:297
  451.8 56.4 %all-gather.42.cloned.1.call-start = ((), (), s32[]{:S(2)}) async-start(), calls=%async_computation.44 | async-start | bytes 2621440 | tf_op jit(solution)/shard_map/all_gather | solution.py:317
  452.5 80.5 %all-gather.34.cloned.1.call-start = ((), (), s32[]{:S(2)}) async-start(), calls=%async_computation.36 | async-start | bytes 2621440 | tf_op jit(solution)/shard_map/all_gather | solution.py:289
  486.3 93.3 %reduce-scatter.49.cloned.1.call-start = ((), (), s32[]{:S(2)}) async-start(), calls=%async_computation.45 | async-start | bytes 2621440 | tf_op jit(solution)/shard_map/reduce_scatter | solution.py:297
  548.1 65.8 %reduce-scatter.41.cloned.1.call-start = ((), (), s32[]{:S(2)}) async-start(), calls=%async_computation.37 | async-start | bytes 2621440 | tf_op jit(solution)/shard_map/reduce_scatter | solution.py:311
  555.0 85.7 %all-gather.44.cloned.1.call-start = ((), (), s32[]{:S(2)}) async-start(), calls=%async_computation.46 | async-start | bytes 2621440 | tf_op jit(solution)/shard_map/all_gather | solution.py:317
  617.9 47.5 %all-gather.38.cloned.1.call-start = ((), (), s32[]{:S(2)}) async-start(), calls=%async_computation.40 | async-start | bytes 2621440 | tf_op jit(solution)/shard_map/all_gather | solution.py:317
  618.5 79.5 %reduce-scatter.51.cloned.1.call-start = ((), (), s32[]{:S(2)}) async-start(), calls=%async_computation.47 | async-start | bytes 2621440 | tf_op jit(solution)/shard_map/reduce_scatter | solution.py:297
  663.8 66.0 %reduce-scatter.45.cloned.1.call-start = ((), (), s32[]{:S(2)}) async-start(), calls=%async_computation.41 | async-start | bytes 2621440 | tf_op jit(solution)/shard_map/reduce_scatter | solution.py:297
  690.6 73.3 %reduce-scatter.35.cloned.1.call-start = ((), (), s32[]{:S(2)}) async-start(), calls=%async_computation.31 | async-start | bytes 2621440 | tf_op jit(solution)/shard_map/reduce_scatter | solution.py:311
  698.0 122.1 %all-gather.40.cloned.1.call-start = ((), (), s32[]{:S(2)}) async-start(), calls=%async_computation.42 | async-start | bytes 2621440 | tf_op jit(solution)/shard_map/all_gather | solution.py:317
  767.6 54.8 %all-gather.46.cloned.1.call-start = ((), (), s32[]{:S(2)}) async-start(), calls=%async_computation.48 | async-start | bytes 2621440 | tf_op jit(solution)/shard_map/all_gather | solution.py:317
  771.0 117.6 %reduce-scatter.77.cloned.1.call-start = ((), (), s32[]{:S(2)}) async-start(), calls=%async_computation.63 | async-start | bytes 2359296
  785.3 172.7 %reduce-scatter.71.cloned.1.call-start = ((), (), s32[]{:S(2)}) async-start(), calls=%async_computation.58 | async-start | bytes 2359296 | tf_op jit(solution)/shard_map/reduce_scatter | solution.py:526
  794.3 227.9 %reduce-scatter.75.cloned.1.call-start = ((), (), s32[]{:S(2)}) async-start(), calls=%async_computation.62 | async-start | bytes 589824
  798.6 288.4 %reduce-scatter.65.cloned.1.call-start = ((), (), s32[]{:S(2)}) async-start(), calls=%async_computation.55 | async-start | bytes 589824 | tf_op jit(solution)/shard_map/reduce_scatter | solution.py:508
  804.0 347.5 %reduce-scatter.67.cloned.1.call-start = ((), (), s32[]{:S(2)}) async-start(), calls=%async_computation.56 | async-start | bytes 589824 | tf_op jit(solution)/shard_map/reduce_scatter | solution.py:511
  811.4 404.7 %reduce-scatter.69.cloned.1.call-start = ((), (), s32[]{:S(2)}) async-start(), calls=%async_computation.57 | async-start | bytes 589824 | tf_op jit(solution)/shard_map/reduce_scatter | solution.py:517
  812.0 437.4 %reduce-scatter.57.cloned.1.call-start = ((), (), s32[]{:S(2)}) async-start(), calls=%async_computation.51 | async-start | bytes 2560000 | tf_op jit(solution)/shard_map/reduce_scatter | solution.py:454
  815.0 468.1 %reduce-scatter.55.cloned.1.call-start = ((), (), s32[]{:S(2)}) async-start(), calls=%async_computation.50 | async-start | bytes 2560000 | tf_op jit(solution)/shard_map/reduce_scatter | solution.py:454
  817.8 530.4 %reduce-scatter.73.cloned.1.call-start = ((), (), s32[]{:S(2)}) async-start(), calls=%async_computation.61 | async-start | bytes 589824
  862.6 550.3 %reduce-scatter.59.cloned.1.call-start = ((), (), s32[]{:S(2)}) async-start(), calls=%async_computation.52 | async-start | bytes 589824 | tf_op jit(solution)/shard_map/reduce_scatter | solution.py:487
  873.0 604.3 %reduce-scatter.61.cloned.1.call-start = ((), (), s32[]{:S(2)}) async-start(), calls=%async_computation.53 | async-start | bytes 589824 | tf_op jit(solution)/shard_map/reduce_scatter | solution.py:493
  873.7 668.1 %reduce-scatter.63.cloned.1.call-start = ((), (), s32[]{:S(2)}) async-start(), calls=%async_computation.54 | async-start | bytes 589824 | tf_op jit(solution)/shard_map/reduce_scatter | solution.py:499
  874.3 701.1 %reduce-scatter.47.cloned.1.call-start = ((), (), s32[]{:S(2)}) async-start(), calls=%async_computation.43 | async-start | bytes 2621440 | tf_op jit(solution)/shard_map/reduce_scatter | solution.py:297
  878.9 730.5 %reduce-scatter.53.cloned.1.call-start = ((), (), s32[]{:S(2)}) async-start(), calls=%async_computation.49 | async-start | bytes 2621440 | tf_op jit(solution)/shard_map/reduce_scatter | solution.py:297
  959.8 325.9 %copy-start.38 = (f32[1,1024,256]{2,1,0:T(8,128)S(1)}, f32[1,1024,256]{2,1,0:T(8,128)}, u32[]{:S(2)}) copy-start(f32[1,1024,256]{2,1,0:T(8,128)} %get-tuple-element.118) | copy-start | bytes 3145732
  959.8 325.9 %copy-start.39 = (f32[1,1024,256]{2,1,0:T(8,128)S(1)}, f32[1,1024,256]{2,1,0:T(8,128)}, u32[]{:S(2)}) copy-start(f32[1,1024,256]{2,1,0:T(8,128)} %get-tuple-element.122) | copy-start | bytes 3145732
  1287.2 322.3 %copy-start.28 = (f32[2,1024,256]{2,1,0:T(8,128)S(1)}, f32[2,1024,256]{2,1,0:T(8,128)}, u32[]{:S(2)}) copy-start(f32[2,1024,256]{2,1,0:T(8,128)} %param.19) | copy-start | bytes 6291460
  1287.2 322.3 %copy-start.66 = (f32[1024]{0:T(1024)S(1)}, f32[1024]{0:T(1024)}, u32[]{:S(2)}) copy-start(f32[1024]{0:T(1024)} %copy-done.65) | copy-start | bytes 12292
  1287.2 322.3 %copy-start.68 = (f32[1024]{0:T(1024)S(1)}, f32[1024]{0:T(1024)}, u32[]{:S(2)}) copy-start(f32[1024]{0:T(1024)} %copy-done.67) | copy-start | bytes 12292
  1287.2 322.3 %copy-start.77 = (f32[256]{0:T(256)S(1)}, f32[256]{0:T(256)}, u32[]{:S(2)}) copy-start(f32[256]{0:T(256)} %param.24) | copy-start | bytes 3076
  1288.6 328.9 %copy-start.72 = (f32[1024]{0:T(1024)S(1)}, f32[1024]{0:T(1024)}, u32[]{:S(2)}) copy-start(f32[1024]{0:T(1024)} %copy-done.71) | copy-start | bytes 12292
  1288.6 328.9 %copy-start.74 = (f32[1024]{0:T(1024)S(1)}, f32[1024]{0:T(1024)}, u32[]{:S(2)}) copy-start(f32[1024]{0:T(1024)} %copy-done.73) | copy-start | bytes 12292
  (88 other events, 729.4 us)
Sparse Core Ops, SparseCore 0:
  20.3 23.1 all-gather.19
  45.6 22.8 all-gather.29
  114.5 29.8 reduce-scatter.30
  147.5 31.4 reduce-scatter.36
  180.4 22.5 all-gather.49
  205.0 22.8 all-gather.31
  229.4 22.5 all-gather.47
  254.1 22.8 all-gather.21
  280.1 31.4 reduce-scatter.38
  314.7 31.4 reduce-scatter.32
  664.0 31.4 reduce-scatter.50
  698.4 31.4 reduce-scatter.44
  732.5 31.4 reduce-scatter.34
Sparse Core Ops, SparseCore 1:
  296.0 47.0 all-gather.27
  345.0 20.9 all-gather.35
  367.5 45.5 all-gather.25
  415.2 21.5 all-gather.23
  451.9 31.3 reduce-scatter.42
  485.5 22.6 all-gather.41
  510.3 22.7 all-gather.33
  548.2 31.3 reduce-scatter.48
  582.5 31.3 reduce-scatter.40
  618.0 22.6 all-gather.43
  642.7 22.7 all-gather.37
  767.7 22.7 all-gather.39
  792.4 22.7 all-gather.45
  818.7 68.1 reduce-scatter.76
  890.9 67.0 reduce-scatter.70
  961.4 60.8 reduce-scatter.74
  1026.0 61.0 reduce-scatter.64
  1090.4 61.0 reduce-scatter.66
  1155.1 61.0 reduce-scatter.68
  1219.3 30.0 reduce-scatter.56
  1252.0 31.0 reduce-scatter.54
  1286.3 61.9 reduce-scatter.72
  1351.9 61.0 reduce-scatter.58
  1416.2 61.0 reduce-scatter.60
  1480.8 61.0 reduce-scatter.62
  1545.0 30.3 reduce-scatter.46
  1578.1 31.3 reduce-scatter.52

commit v2 on v1

v2 whole, which is shorter than its diff:
```python
import functools

import jax
import jax.numpy as jnp
from jax import lax
from jax.experimental import pallas as pl
from jax.experimental.pallas import tpu as pltpu
from jax.sharding import PartitionSpec as P

NEG_FILL = -1000000000.0
BLOCK = 256
PAIR = 128
LOW = jnp.bfloat16
WIDE = jnp.float32


def dot_tn(left, right):
    return lax.dot_general(left, right, (((0,), (0,)), ((), ())), preferred_element_type=jnp.float32)


def dot_nt(left, right):
    return lax.dot_general(left, right, (((1,), (1,)), ((), ())), preferred_element_type=jnp.float32)


def dot_nn(left, right):
    return lax.dot_general(left, right, (((1,), (0,)), ((), ())), preferred_element_type=jnp.float32)


def head_mask(head, head_size):
    lane = lax.broadcasted_iota(jnp.int32, (1, PAIR), 1)
    low = head * head_size
    return ((lane >= low) & (lane < low + head_size)).astype(jnp.float32)


def key_blocks(q_block, key_count, self_mode, prefix_blocks):
    total = key_count // BLOCK
    return min(total, max(q_block + 1, prefix_blocks)) if self_mode else total


def forward_kernel(self_mode, q_count, key_count, key_valid, head_size, prefix_blocks, *refs):
    if self_mode:
        cut_ref, vec_ref, q_ref, k_ref, v_ref, o_ref, rest_ref, lse_ref, band = refs
    else:
        q_ref, k_ref, v_ref, o_ref, rest_ref, lse_ref = refs
    head = pl.program_id(1)
    mask = head_mask(head, head_size)
    mask_low = mask.astype(jnp.bfloat16)
    if self_mode:
        wide = jnp.broadcast_to(vec_ref[0], (BLOCK, band.shape[1]))
        band[...] = pltpu.roll(wide, 0, 1, stride=1, stride_axis=0)
        cut = cut_ref[0]
    base = q_count - BLOCK
    col = lax.broadcasted_iota(jnp.int32, (BLOCK, BLOCK), 1)
    row = lax.broadcasted_iota(jnp.int32, (BLOCK, BLOCK), 0)
    for qb in range(q_count // BLOCK):
        q_rows = pl.ds(qb * BLOCK, BLOCK)
        query = q_ref[q_rows, :] * mask_low
        parts = []
        for kb in range(key_blocks(qb, key_count, self_mode, prefix_blocks)):
            s = dot_nt(query, k_ref[pl.ds(kb * BLOCK, BLOCK), :])
            if self_mode:
                s = s + band[:, pl.ds((kb - qb) * BLOCK + base, BLOCK)]
                if kb >= qb:
                    limit = jnp.maximum(row + qb * BLOCK, cut - 1)
                    s = jnp.where(col + kb * BLOCK <= limit, s, NEG_FILL)
            elif (kb + 1) * BLOCK > key_valid:
                s = jnp.where(col + kb * BLOCK < key_valid, s, NEG_FILL)
            parts.append(s)
        top = functools.reduce(jnp.maximum, [jnp.max(s, axis=1, keepdims=True) for s in parts])
        total = jnp.zeros((BLOCK, 1), jnp.float32)
        mixed = jnp.zeros((BLOCK, PAIR), jnp.float32)
        for kb, s in enumerate(parts):
            e = jnp.exp(s - top)
            total = total + jnp.sum(e, axis=1, keepdims=True)
            mixed = mixed + dot_nn(e.astype(jnp.bfloat16), v_ref[pl.ds(kb * BLOCK, BLOCK), :])
        mixed = mixed * (mask / total)
        mixed_low = mixed.astype(jnp.bfloat16)
        rest = (mixed - mixed_low.astype(jnp.float32)).astype(jnp.bfloat16)

        @pl.when(head == 0)
        def _():
            o_ref[q_rows, :] = mixed_low
            rest_ref[q_rows, :] = rest

        @pl.when(head > 0)
        def _():
            o_ref[q_rows, :] += mixed_low
            rest_ref[q_rows, :] += rest

        log_total = jnp.broadcast_to(top + jnp.log(total), (BLOCK, PAIR))
        lse_ref[0, :, q_rows] = log_total.T[:1]


def backward_kernel(self_mode, q_count, key_count, key_valid, head_size, prefix_blocks, *refs):
    if self_mode:
        cut_ref, vec_ref, q_ref, k_ref, v_ref, o_ref, rest_ref, do_ref, lse_ref = refs[:9]
        dq_ref, dk_ref, dv_ref, diag_ref, kt, dqt, dk_acc, dv_acc, band, acc = refs[9:]
    else:
        q_ref, k_ref, v_ref, o_ref, rest_ref, do_ref, lse_ref = refs[:7]
        dq_ref, dk_ref, dv_ref, kt, dqt, dk_acc, dv_acc = refs[7:]
    head = pl.program_id(1)
    mask = head_mask(head, head_size)
    mask_low = mask.astype(jnp.bfloat16)
    base = q_count - BLOCK

    @pl.when(head == 0)
    def _():
        kt[...] = k_ref[...].T
        dk_acc[...] = jnp.zeros_like(dk_acc)
        dv_acc[...] = jnp.zeros_like(dv_acc)

    if self_mode:
        wide = jnp.broadcast_to(vec_ref[0], (BLOCK, band.shape[1]))
        band[...] = pltpu.roll(wide, 0, 1, stride=1, stride_axis=0)
        acc[...] = jnp.zeros_like(acc)
        cut = cut_ref[0]
    col = lax.broadcasted_iota(jnp.int32, (BLOCK, BLOCK), 1)
    row = lax.broadcasted_iota(jnp.int32, (BLOCK, BLOCK), 0)
    head_rows = pl.ds(pl.multiple_of(head * head_size, head_size), head_size)
    key_t = kt[head_rows, :]
    for qb in range(q_count // BLOCK):
        q_rows = pl.ds(qb * BLOCK, BLOCK)
        query = q_ref[q_rows, :] * mask_low
        grad = do_ref[q_rows, :] * mask_low
        mixed = o_ref[q_rows, :].astype(jnp.float32) + rest_ref[q_rows, :].astype(jnp.float32)
        product = grad.astype(jnp.float32) * mixed
        delta = jnp.sum(product.T, axis=0, keepdims=True)
        log_total = lse_ref[0, :, q_rows]
        dqt_sum = jnp.zeros((head_size, BLOCK), jnp.float32)
        for kb in range(key_blocks(qb, key_count, self_mode, prefix_blocks)):
            k_rows = pl.ds(kb * BLOCK, BLOCK)
            s = dot_nt(k_ref[k_rows, :], query)
            dp = dot_nt(v_ref[k_rows, :], grad)
            if self_mode:
                span = pl.ds((qb - kb) * BLOCK + base, BLOCK)
                s = s + band[:, span]
                if kb >= qb:
                    limit = jnp.maximum(col + qb * BLOCK, cut - 1)
                    s = jnp.where(row + kb * BLOCK <= limit, s, NEG_FILL)
            elif (kb + 1) * BLOCK > key_valid:
                s = jnp.where(row + kb * BLOCK < key_valid, s, NEG_FILL)
            p = jnp.exp(s - log_total)
            ds = p * (dp - delta)
            ds_low = ds.astype(jnp.bfloat16)
            if self_mode:
                acc[:, span] += ds
            dv_acc[k_rows, :] += dot_nn(p.astype(jnp.bfloat16), grad)
            dk_acc[k_rows, :] += dot_nn(ds_low, query)
            dqt_sum = dqt_sum + dot_nn(key_t[:, kb * BLOCK : (kb + 1) * BLOCK], ds_low)
        dqt[head_rows, q_rows] = dqt_sum
    if self_mode:
        size = BLOCK
        fold = acc[...]
        lanes = fold.shape[1]
        while size > 8:
            size //= 2
            fold = fold[:size] + pltpu.roll(fold[size:], lanes - size, 1)
        diag_ref[0] = fold

    @pl.when(head == pl.num_programs(1) - 1)
    def _():
        dq_ref[...] = dqt[...].T.astype(jnp.bfloat16)
        dk_ref[...] = dk_acc[...].astype(jnp.bfloat16)
        dv_ref[...] = dv_acc[...].astype(jnp.bfloat16)


def lane_block(rows, offset):
    return pl.BlockSpec((rows, PAIR), lambda p, h: (0, p + offset))


def attention_forward(q_arr, k_arr, v_arr, offsets, head_count, head_size, key_valid, vec=None, cut=None, prefix_blocks=0):
    q_count, key_count = q_arr.shape[0], k_arr.shape[0]
    self_mode = vec is not None
    per = PAIR // head_size
    pairs = head_count // per
    in_specs = [
        lane_block(q_count, offsets[0]),
        lane_block(key_count, offsets[1]),
        lane_block(key_count, offsets[2]),
    ]
    args = [q_arr, k_arr, v_arr]
    scratch = []
    if self_mode:
        lanes = vec.shape[-1]
        in_specs = [
            pl.BlockSpec(memory_space=pltpu.SMEM),
            pl.BlockSpec((1, 1, lanes), lambda p, h: (p * per + h, 0, 0)),
        ] + in_specs
        args = [cut, vec] + args
        scratch = [pltpu.VMEM((BLOCK, lanes), jnp.float32)]
    return pl.pallas_call(
        functools.partial(forward_kernel, self_mode, q_count, key_count, key_valid, head_size, prefix_blocks),
        out_shape=(
            jax.ShapeDtypeStruct((q_count, head_count * head_size), jnp.bfloat16),
            jax.ShapeDtypeStruct((q_count, head_count * head_size), jnp.bfloat16),
            jax.ShapeDtypeStruct((head_count, 1, q_count), jnp.float32),
        ),
        grid=(pairs, per),
        in_specs=in_specs,
        out_specs=(
            lane_block(q_count, 0),
            lane_block(q_count, 0),
            pl.BlockSpec((1, 1, q_count), lambda p, h: (p * per + h, 0, 0)),
        ),
        scratch_shapes=scratch,
        compiler_params=pltpu.CompilerParams(vmem_limit_bytes=40 << 20),
        cost_estimate=pl.CostEstimate(
            flops=4 * head_count * q_count * key_count * PAIR,
            bytes_accessed=4 * head_count * q_count * head_size * 2,
            transcendentals=head_count * q_count * key_count,
        ),
        name="self_forward" if self_mode else "cross_forward",
    )(*args)


def attention_backward(q_arr, k_arr, v_arr, offsets, out, rest, grad, log_total, head_count, head_size, key_valid, vec=None, cut=None, prefix_blocks=0):
    q_count, key_count = q_arr.shape[0], k_arr.shape[0]
    self_mode = vec is not None
    per = PAIR // head_size
    pairs = head_count // per
    width = head_count * head_size
    in_specs = [
        lane_block(q_count, offsets[0]),
        lane_block(key_count, offsets[1]),
        lane_block(key_count, offsets[2]),
        lane_block(q_count, 0),
        lane_block(q_count, 0),
        lane_block(q_count, 0),
        pl.BlockSpec((1, 1, q_count), lambda p, h: (p * per + h, 0, 0)),
    ]
    args = [q_arr, k_arr, v_arr, out, rest, grad, log_total]
    scratch = [
        pltpu.VMEM((PAIR, key_count), jnp.bfloat16),
        pltpu.VMEM((PAIR, q_count), jnp.float32),
        pltpu.VMEM((key_count, PAIR), jnp.float32),
        pltpu.VMEM((key_count, PAIR), jnp.float32),
    ]
    out_shape = [
        jax.ShapeDtypeStruct((q_count, width), jnp.bfloat16),
        jax.ShapeDtypeStruct((key_count, width), jnp.bfloat16),
        jax.ShapeDtypeStruct((key_count, width), jnp.bfloat16),
    ]
    out_specs = [lane_block(q_count, 0), lane_block(key_count, 0), lane_block(key_count, 0)]
    if self_mode:
        lanes = vec.shape[-1]
        in_specs = [
            pl.BlockSpec(memory_space=pltpu.SMEM),
            pl.BlockSpec((1, 1, lanes), lambda p, h: (p * per + h, 0, 0)),
        ] + in_specs
        args = [cut, vec] + args
        scratch += [pltpu.VMEM((BLOCK, lanes), jnp.float32), pltpu.VMEM((BLOCK, lanes), jnp.float32)]
        out_shape.append(jax.ShapeDtypeStruct((head_count, 8, lanes), jnp.float32))
        out_specs.append(pl.BlockSpec((1, 8, lanes), lambda p, h: (p * per + h, 0, 0)))
    return pl.pallas_call(
        functools.partial(backward_kernel, self_mode, q_count, key_count, key_valid, head_size, prefix_blocks),
        out_shape=tuple(out_shape),
        grid=(pairs, per),
        in_specs=in_specs,
        out_specs=tuple(out_specs),
        scratch_shapes=scratch,
        compiler_params=pltpu.CompilerParams(vmem_limit_bytes=40 << 20),
        cost_estimate=pl.CostEstimate(
            flops=10 * head_count * q_count * key_count * PAIR,
            bytes_accessed=8 * head_count * q_count * head_size * 2,
            transcendentals=head_count * q_count * key_count,
        ),
        name="self_backward" if self_mode else "cross_backward",
    )(*args)


def smooth_act(values):
    return jax.nn.gelu(values, approximate=True)


class Layout:
    def __init__(self):
        self.col = lax.axis_size("col")
        self.team = self.col // 2
        self.bits = self.team.bit_length() - 1
        self.rows = lax.axis_size("row")
        self.index = lax.axis_index("col")
        self.micro = self.index // self.team
        self.member = self.index % self.team
        self.dp = lax.axis_index("dp")
        self.row = lax.axis_index("row")
        self.far_index = (1 - self.micro) * self.team + self.member

    def swap_half(self, array):
        return lax.ppermute(array, "col", [(i, (i + self.team) % self.col) for i in range(self.col)])

    def swap_bit(self, array, bit):
        return lax.ppermute(array, "col", [(i, i ^ (1 << bit)) for i in range(self.col)])

    def swap_dp(self, array):
        return lax.ppermute(array, "dp", [(0, 1), (1, 0)])

    def swap_row(self, array, bit):
        return lax.ppermute(array, "row", [(i, i ^ (1 << bit)) for i in range(self.rows)])

    def bit_of(self, bit):
        return (self.member >> bit) & 1

    def own(self, pair):
        return jnp.where(self.micro == 0, pair[0], pair[1])

    def other(self, pair):
        return jnp.where(self.micro == 0, pair[1], pair[0])

    def in_order(self, own, other):
        return jnp.stack((jnp.where(self.micro == 0, own, other), jnp.where(self.micro == 0, other, own)))

    def team_gather(self, array):
        parts = [array]
        for bit in range(self.bits):
            sent = parts[0] if len(parts) == 1 else jnp.stack(parts)
            got = self.swap_bit(sent, bit)
            got = [got] if len(parts) == 1 else [got[i] for i in range(len(parts))]
            low = self.bit_of(bit) == 0
            parts = [jnp.where(low, mine, far) for mine, far in zip(parts, got)] + [
                jnp.where(low, far, mine) for mine, far in zip(parts, got)
            ]
        return parts

    def team_sum(self, array):
        for bit in range(self.bits):
            array = array + self.swap_bit(array.astype(LOW), bit).astype(WIDE)
        return array

    def team_scatter(self, arrays, axis, kind=LOW):
        for bit in reversed(range(self.bits)):
            half = arrays[0].shape[axis] // 2
            mine = self.bit_of(bit)
            keep = [lax.dynamic_slice_in_dim(a, mine * half, half, axis) for a in arrays]
            sent = [lax.dynamic_slice_in_dim(a, (1 - mine) * half, half, axis) for a in arrays]
            got = self.swap_bit(jnp.concatenate(sent).astype(kind), bit).astype(WIDE)
            starts = [sum(k.shape[0] for k in keep[:i]) for i in range(len(keep))]
            arrays = [k + got[at : at + k.shape[0]] for k, at in zip(keep, starts)]
        return arrays

    def half_columns(self, array):
        size = array.shape[1] // 2
        return [
            lax.dynamic_slice_in_dim(array, start * size, size, 1)
            for start in (self.micro, 1 - self.micro)
        ]

    def full_width(self, own, other):
        low, high = jnp.where(self.micro == 0, own, other), jnp.where(self.micro == 0, other, own)
        parts = self.team_gather(jnp.stack((low, high)))
        return jnp.concatenate([part[half] for half in range(2) for part in parts], axis=1)

    def sum_rows(self, array):
        half = array.shape[0] // 2
        keep = lax.dynamic_slice_in_dim(array, self.dp * half, half, 0)
        sent = lax.dynamic_slice_in_dim(array, (1 - self.dp) * half, half, 0)
        array = keep.astype(WIDE) + self.swap_dp(sent.astype(LOW)).astype(WIDE)
        columns = array.shape[1]
        bits = self.rows.bit_length() - 1
        for bit in range(bits):
            left = 1 << (bits - bit - 1)
            pieces = array.reshape(left, 2, -1, columns)
            mine = (self.row >> bit) & 1
            keep = lax.dynamic_index_in_dim(pieces, mine, 1, keepdims=False)
            sent = lax.dynamic_index_in_dim(pieces, 1 - mine, 1, keepdims=False)
            array = keep + self.swap_row(sent.astype(LOW), bit).astype(WIDE)
            array = array.reshape(-1, columns)
        return array

    def sum_all(self, array):
        array = array + self.swap_dp(array)
        for bit in range(self.rows.bit_length() - 1):
            array = array + self.swap_row(array, bit)
        return array


def tie(*arrays):
    return lax.optimization_barrier(arrays)


def rms(rows):
    return lax.rsqrt(jnp.mean(rows * rows, axis=1, keepdims=True) + 1e-06)


def norm_backward(grad, rows, scale, gain):
    scaled = grad * gain
    inner = jnp.mean(scaled * rows, axis=1, keepdims=True)
    return scale * scaled - rows * (scale * scale * scale * inner)


def gain_part(grad, rows, scale):
    return jnp.sum(grad * (rows * scale), axis=0)


def body(
    residual_in,
    encoder_out,
    prefix_len,
    bucket_table,
    cotangent,
    norm_self,
    norm_cross,
    norm_ffn,
    self_query,
    self_key,
    self_value,
    self_out,
    cross_query,
    cross_key,
    cross_value,
    cross_out,
    ffn_in,
    ffn_out,
    rel_bias,
):
    place = Layout()
    team = place.team
    micro_count, rows, width = residual_in.shape
    assert micro_count == 2 and prefix_len.shape[1] == 1 and lax.axis_size("dp") == 2
    memory_len = encoder_out.shape[1]
    heads = rel_bias.shape[1]
    inner = self_query.shape[1]
    head_size = inner // heads
    units = ffn_in.shape[1]
    bias_rows = rel_bias.shape[0]
    buckets = bias_rows * place.rows
    pairs = inner // PAIR
    model = width * place.col
    cut = place.own(prefix_len)

    resid_low = residual_in.astype(LOW)
    resid_far = place.swap_half(place.other(resid_low))
    resid = place.full_width(place.own(resid_low), resid_far).astype(WIDE)
    gain_own = jnp.stack((norm_self, norm_cross, norm_ffn))
    gain_full = place.full_width(gain_own, place.swap_half(gain_own))
    gains = [gain_full[i : i + 1] for i in range(3)]

    def gather_half(blocks, extra=None):
        local = jnp.concatenate([block.astype(LOW) for block in blocks], axis=1)
        half = local.shape[0] // 2
        mine = jnp.where(place.dp == 0, local[:half], local[half:])
        if extra is not None:
            mine = jnp.concatenate((mine, extra))
        return lax.all_gather(mine, "row", axis=0, tiled=True)

    def join(first, second):
        count = model // (2 * place.rows)
        first, second = (a.reshape(place.rows, -1, a.shape[1])[:, :count] for a in (first, second))
        low = jnp.where(place.dp == 0, first, second)
        high = jnp.where(place.dp == 0, second, first)
        return jnp.concatenate((low, high), axis=1).reshape(model, -1)

    spare = jnp.pad(rel_bias.reshape(-1), (0, 8 * 3 * inner - rel_bias.size)).astype(LOW)
    near = gather_half((self_query, self_key, self_value), spare.reshape(8, -1))
    far = place.swap_half(near)
    qkv_weights = [join(near, place.swap_dp(near)), join(far, place.swap_dp(far))]
    tables = [
        side.reshape(place.rows, -1, 3 * inner)[:, -8:].reshape(place.rows, -1)[:, : rel_bias.size]
        .reshape(buckets, heads).astype(WIDE)
        for side in (near, far)
    ]
    mid_near = gather_half((self_out.T, cross_query, cross_key, cross_value, cross_out.T))
    mid_far = place.swap_half(mid_near)
    mid_weights = [join(mid_near, place.swap_dp(mid_near)), join(mid_far, place.swap_dp(mid_far))]
    out_weights = [w[:, :inner] for w in mid_weights]
    cross_q_weights = [w[:, inner : 2 * inner] for w in mid_weights]
    cross_kv_weights = [w[:, 2 * inner : 4 * inner] for w in mid_weights]
    cross_out_weights = [w[:, 4 * inner :] for w in mid_weights]
    ffn_near = gather_half((ffn_in, ffn_out.T))

    bucket_ids = jnp.arange(buckets, dtype=jnp.int32)

    def onehot(index):
        index = jnp.roll(jnp.pad(index, (0, 1), constant_values=-1), 1 - BLOCK)
        return (index[:, None] == bucket_ids[None, :]).astype(WIDE)

    def bands(index):
        return [
            jnp.dot(index, table, precision=lax.Precision.HIGHEST).T.reshape(heads, 1, -1)
            for table in tables
        ]

    back_onehot = onehot(bucket_table[::-1])
    bands_forward = bands(onehot(bucket_table))
    bands_backward = bands(back_onehot)
    prefix_blocks = -(-(rows // 2) // BLOCK)

    memory_low = encoder_out.astype(LOW)
    memory_far = place.swap_half(place.other(memory_low))
    memory = place.full_width(place.own(memory_low), memory_far)
    memory = jnp.pad(memory, ((0, -memory_len % BLOCK), (0, 0)))
    cot_low = cotangent.astype(LOW)
    cot_far = place.swap_half(cot_low)

    scale_one = rms(resid)
    normed_one = (resid * scale_one * gains[0]).astype(LOW)
    qkv, self_mix = [], []
    for weight, band in zip(qkv_weights, bands_forward):
        qkv.append(dot_nn(normed_one, weight).astype(LOW))
        self_mix.append(
            attention_forward(
                qkv[-1], qkv[-1], qkv[-1], (0, pairs, 2 * pairs), heads, head_size, rows, band, cut,
                prefix_blocks,
            )
        )
    part = sum(dot_nt(mix[0], w) for mix, w in zip(self_mix, out_weights))
    part, ffn_near, memory = tie(part, ffn_near, memory)
    added = place.team_sum(part)
    resid_one = resid + added
    ffn_far = place.swap_dp(ffn_near)

    scale_two = rms(resid_one)
    normed_two = (resid_one * scale_two * gains[1]).astype(LOW)
    cross_q, cross_kv, cross_mix = [], [], []
    for q_weight, kv_weight in zip(cross_q_weights, cross_kv_weights):
        cross_kv.append(dot_nn(memory, kv_weight).astype(LOW))
        cross_q.append(dot_nn(normed_two, q_weight).astype(LOW))
        cross_mix.append(
            attention_forward(
                cross_q[-1], cross_kv[-1], cross_kv[-1], (0, 0, pairs), heads, head_size, memory_len
            )
        )
    part = sum(dot_nt(mix[0], w) for mix, w in zip(cross_mix, cross_out_weights))
    part, ffn_far, cot_far = tie(part, ffn_far, cot_far)
    added_two = place.team_sum(part)
    added = added + added_two
    resid_two = resid_one + added_two
    cot_own = place.full_width(place.own(cot_low), place.own(cot_far))
    cot_other = place.full_width(place.other(cot_low), place.other(cot_far))

    ffn_weights = join(ffn_near, ffn_far)
    weight_in, weight_out = ffn_weights[:, :units], ffn_weights[:, units:]
    scale_three = rms(resid_two)
    normed_three = (resid_two * scale_three * gains[2]).astype(LOW)
    chunk = rows // team
    sent = lax.dynamic_slice_in_dim(normed_three, place.member * chunk, chunk, axis=0)
    got = place.swap_half(sent)

    def feed_forward(normed, cot):
        act_values, act_pull = jax.vjp(smooth_act, dot_nn(normed, weight_in))
        return act_values.astype(LOW), act_pull(dot_nn(cot, weight_out))[0].astype(LOW)

    act_own, pre_own = feed_forward(normed_three, cot_own)
    got, act_own, pre_own = tie(got, act_own, pre_own)
    far_three = jnp.concatenate(place.team_gather(got))
    act_other, pre_other = feed_forward(far_three, cot_other)
    (piece,) = place.team_scatter([dot_nt(pre_other, weight_in)], 0)
    got = place.swap_half(piece.astype(LOW))
    (piece,) = place.team_scatter([dot_nt(pre_own, weight_in)], 0)

    def reduce_rows(array):
        return lax.psum_scatter(array.astype(LOW), ("dp", "row"), scatter_dimension=0, tiled=True)

    ffn_pack = jnp.concatenate(
        (
            dot_tn(normed_three, pre_own) + dot_tn(far_three, pre_other),
            dot_tn(cot_own, act_own) + dot_tn(cot_other, act_other),
        ),
        axis=1,
    ).astype(LOW)
    tops = [dot_nt(act, weight_out) for act in (act_own, act_other)]
    got, ffn_pack, *tops = tie(got, ffn_pack, *tops)
    grad_three = place.team_gather((piece + got.astype(WIDE)).astype(LOW))
    grad_three = jnp.concatenate(grad_three).astype(WIDE)
    ffn_grads = reduce_rows(ffn_pack)

    gain_three = gain_part(grad_three, resid_two, scale_three)
    grad_two = norm_backward(grad_three, resid_two, scale_three, gains[2])
    grad_low = (cot_own.astype(WIDE) + grad_two).astype(LOW)

    columns = [part for top in tops for part in place.half_columns(top)]
    own_keep, own_send, other_keep, other_send = place.team_scatter(columns, 1)
    own_keep = own_keep + lax.dynamic_slice_in_dim(added, place.index * width, width, 1)
    own_send = own_send + lax.dynamic_slice_in_dim(added, place.far_index * width, width, 1)
    top_got = place.swap_half(jnp.stack((other_send, own_send)).astype(LOW))

    cross_grads = [None, None]
    cross_packs = [None, None]
    cross_got = None
    for side in (1, 0):
        mix, rest, log_total = cross_mix[side]
        grad_mix = dot_nn(grad_low, cross_out_weights[side]).astype(LOW)
        dq, dk, dv = attention_backward(
            cross_q[side], cross_kv[side], cross_kv[side], (0, 0, pairs), mix, rest, grad_mix,
            log_total, heads, head_size, memory_len,
        )
        if side == 0:
            dq, top_got = tie(dq, top_got)
        cross_grads[side] = (dq, jnp.concatenate((dk, dv), axis=1))
        cross_packs[side] = jnp.concatenate(
            (
                dot_tn(normed_two, dq),
                dot_tn(memory, cross_grads[side][1]),
                dot_tn(grad_low, mix),
            ),
            axis=1,
        ).astype(LOW)
        if side == 1:
            cross_got = place.swap_half(cross_packs[1])
    layer_out = residual_in + place.in_order(
        own_keep + top_got[0].astype(WIDE), other_keep + top_got[1].astype(WIDE)
    )
    grad_part = sum(dot_nt(cross_grads[side][0], cross_q_weights[side]) for side in (1, 0))
    memory_part = sum(dot_nt(cross_grads[side][1], cross_kv_weights[side]) for side in (1, 0))
    gain_two = gain_part(grad_part, resid_one, scale_two)
    grad_one = grad_two + norm_backward(
        place.team_sum(grad_part), resid_one, scale_two, gains[1]
    )

    grad_low = (cot_own.astype(WIDE) + grad_one).astype(LOW)
    cross_got, grad_low = tie(cross_got, grad_low)
    cross_total = reduce_rows(cross_packs[0].astype(WIDE) + cross_got.astype(WIDE))
    memory_keep, memory_send = place.team_scatter(place.half_columns(memory_part), 1)
    memory_got = place.swap_half(memory_send[:memory_len].astype(LOW))
    self_grads = [None, None]
    out_packs = [dot_tn(grad_low, mix[0]).astype(LOW) for mix in self_mix]
    out_got = place.swap_half(out_packs[1])
    self_packs = [None, None]
    diagonals = [None, None]
    for side in (1, 0):
        mix, rest, log_total = self_mix[side]
        grad_mix = dot_nn(grad_low, out_weights[side]).astype(LOW)
        dq, dk, dv, diagonals[side] = attention_backward(
            qkv[side], qkv[side], qkv[side], (0, pairs, 2 * pairs), mix, rest, grad_mix,
            log_total, heads, head_size, rows, bands_backward[side], cut, prefix_blocks,
        )
        if side == 0:
            dq, self_got, out_got, memory_got = tie(dq, self_got, out_got, memory_got)
        self_grads[side] = jnp.concatenate((dq, dk, dv), axis=1)
        self_packs[side] = dot_tn(normed_one, self_grads[side]).astype(LOW)
        if side == 1:
            self_got = place.swap_half(self_packs[1])
    grad_memory = place.in_order(memory_keep[:memory_len], memory_got.astype(WIDE))
    self_total = jnp.concatenate(
        (
            self_packs[0].astype(WIDE) + self_got.astype(WIDE),
            out_packs[0].astype(WIDE) + out_got.astype(WIDE),
        ),
        axis=1,
    )
    self_total = place.sum_rows(self_total)
    grad_part = sum(dot_nt(self_grads[side], qkv_weights[side]) for side in (1, 0))
    gain_one = gain_part(grad_part, resid, scale_one)
    grad_zero = grad_one + norm_backward(place.team_sum(grad_part), resid, scale_one, gains[0])
    zero_send = lax.dynamic_slice_in_dim(grad_zero, place.far_index * width, width, 1)
    zero_keep = lax.dynamic_slice_in_dim(grad_zero, place.index * width, width, 1)
    zero_got = place.swap_half(zero_send.astype(LOW)).astype(WIDE)
    grad_residual = cotangent + place.in_order(zero_keep, zero_got)

    folded = [
        sum(jnp.roll(diag[:, i], -i, axis=1) for i in range(8)) for diag in diagonals
    ]
    bias_grads = [
        jnp.dot(back_onehot.T, fold.T, precision=lax.Precision.HIGHEST) for fold in folded
    ]
    gain_sums = jnp.stack((gain_one, gain_two, gain_three / team))
    gain_keep, gain_send = place.team_scatter(place.half_columns(gain_sums), 1, WIDE)
    small_send = jnp.concatenate((gain_send.reshape(-1), bias_grads[1].reshape(-1)))
    small_keep = jnp.concatenate((gain_keep.reshape(-1), bias_grads[0].reshape(-1)))
    small = place.sum_all(small_keep + place.swap_half(small_send))
    gain_sums = small[: 3 * width].reshape(3, width)
    part_rows = buckets // (2 * place.rows)
    bias_sum = lax.dynamic_slice_in_dim(
        small[3 * width :].reshape(buckets, heads),
        (place.dp * place.rows + place.row) * part_rows,
        part_rows,
        axis=0,
    )

    def columns_of(array, first, last):
        return array[:, first:last].astype(WIDE)

    return (
        layer_out,
        grad_residual,
        grad_memory,
        gain_sums[0],
        gain_sums[1],
        gain_sums[2],
        columns_of(self_total, 0, inner),
        columns_of(self_total, inner, 2 * inner),
        columns_of(self_total, 2 * inner, 3 * inner),
        columns_of(self_total, 3 * inner, 4 * inner).T,
        columns_of(cross_total, 0, inner),
        columns_of(cross_total, inner, 2 * inner),
        columns_of(cross_total, 2 * inner, 3 * inner),
        columns_of(cross_total, 3 * inner, 4 * inner).T,
        columns_of(ffn_grads, 0, units),
        columns_of(ffn_grads, units, 2 * units).T,
        bias_sum,
    )


def solution(mesh):
    in_specs = (
        P(None, ("dp", "row"), "col"),
        P(None, ("dp", "row"), "col"),
        P(None, ("dp", "row")),
        P(),
        P(None, ("dp", "row"), "col"),
        P("col"),
        P("col"),
        P("col"),
        P("row", "col"),
        P("row", "col"),
        P("row", "col"),
        P("col", "row"),
        P("row", "col"),
        P("row", "col"),
        P("row", "col"),
        P("col", "row"),
        P("row", "col"),
        P("col", "row"),
        P("row", "col"),
    )
    out_specs = (
        P(None, ("dp", "row"), "col"),
        P(None, ("dp", "row"), "col"),
        P(None, ("dp", "row"), "col"),
        P("col"),
        P("col"),
        P("col"),
        P(("dp", "row"), "col"),
        P(("dp", "row"), "col"),
        P(("dp", "row"), "col"),
        P("col", ("dp", "row")),
        P(("dp", "row"), "col"),
        P(("dp", "row"), "col"),
        P(("dp", "row"), "col"),
        P("col", ("dp", "row")),
        P(("dp", "row"), "col"),
        P("col", ("dp", "row")),
        P(("dp", "row"), "col"),
    )
    return jax.shard_map(body, mesh=mesh, in_specs=in_specs, out_specs=out_specs, check_vma=False)
```

time: 1660 us -> 707 us (0.43)
  waiting for transfers between devices: 1050 us -> 170 us
  blocking collectives: 219 us -> 29.5 us
  other arithmetic: 57.1 us -> 130 us
  local copies, waits for them, and re-layouts: 50.1 us -> 96.7 us
  starting transfers between devices: 3.75 us -> 35.5 us
  matrix products: 144 us -> 113 us
    reduce_scatter x21 -> x0, waiting for transfers between devices: 805 us -> none  [the longest x6 153 us: norm_backward(): lax.psum_scatter(grad_part.astype(jnp.bfloat16), 'col', scatter_dimension...]
    ppermute x0 -> x42, waiting for transfers between devices: none -> 168 us  [the longest x15 119 us: swap_half(): lax.ppermute(array, 'col', [(i, (i + self.team) % self.col) for i in rang...]
    all_gather x16 -> x2, waiting for transfers between devices: 138 us -> 0.02 us  [gather_half(): return lax.all_gather(mine, 'row', axis=0, tiled=True)]
    all_gather x9 -> x1, blocking collectives: 137 us -> 29.5 us  [gather_half(): return lax.all_gather(mine, 'row', axis=0, tiled=True)]
    unnamed x43 -> x6, waiting for transfers between devices: 105 us -> 1.95 us
    psum x7 -> x0, blocking collectives: 60.1 us -> none  [the longest x1 22.2 us: body(): lax.psum((gain_sums[0], gain_sums[1], gain_sums[2]), ('dp', 'row'))]
    ppermute x0 -> x42, starting transfers between devices: none -> 35.3 us  [the longest x15 16.2 us: swap_half(): lax.ppermute(array, 'col', [(i, (i + self.team) % self.col) for i in rang...]
    dot_general x44 -> x48, matrix products: 144 us -> 113 us  [the longest x14 41.2 us: dot_nt(): lax.dot_general(left, right, (((1,), (1,)), ((), ())), preferred_element_...]
  transfers between devices with their start and end apart: 40 -> 46, of which waited for: 29 -> 17; matrix products, arithmetic and copies ran while one was open for 11% -> 42% of each run, Pallas kernels for 7% -> 15%
where the time goes in v2:
time: 707 us; the launch traced here: 701 us
  waiting for transfers between devices  170 us (24%)
  other arithmetic  130 us (18%)
  matrix products  113 us (16%)
  Pallas kernels  108 us (15%)
  local copies, waits for them, and re-layouts  96.7 us (14%)
  starting transfers between devices  35.5 us (5%)
  blocking collectives  29.5 us (4%)
  between operations  18.1 us (3%)
    ppermute x15, waiting for transfers between devices, swap_half(): lax.ppermute(array, 'col', [(i, (i + self.team) % self.col) for i in rang...  119 us
    pallas_call x4, Pallas kernels, attention_backward(): pl.pallas_call(functools.partial(backward_kernel, self_mode, q_count, key...  63.1 us
    unnamed x322, local copies, waits for them, and re-layouts  47.4 us
    pallas_call x4, Pallas kernels, attention_forward(): pl.pallas_call(functools.partial(forward_kernel, self_mode, q_count, key_...  44.6 us
    dot_general x14, matrix products, dot_nt(): lax.dot_general(left, right, (((1,), (1,)), ((), ())), preferred_element_...  41.2 us
    dot_general x14, matrix products, dot_nn(): lax.dot_general(left, right, (((1,), (0,)), ((), ())), preferred_element_...  34.4 us
    dot_general x14, matrix products, dot_tn(): lax.dot_general(left, right, (((0,), (0,)), ((), ())), preferred_element_...  33.8 us
    ppermute x7, waiting for transfers between devices, swap_dp(): return lax.ppermute(array, 'dp', [(0, 1), (1, 0)])  31.8 us
  transfers between devices with their start and end apart: 46, of which 17 were waited for; matrix products, arithmetic and copies ran while one was open for 42% of the time, Pallas kernels for 15%

profile of v2, /device:TPU:0, one launch (start us, length us, event | category | flops | bytes accessed | tf_op | source)
XLA Modules:
  0.0 700.5 jit_solution(11602915897267994240)
XLA Ops:
  14.5 29.5 %all_gather.9 = bf16[544,768]{1,0:T(8,128)(2,1)} all-gather(bf16[136,768]{1,0:T(8,128)(2,1)S(1)} %pad_maximum_fusion.26), channel_id=1, replica_groups=mesh['dp'=2,'row'=4,'col'=4] {'row'}, dimensions={0}, use_global_device_ids=true | all-gather | bytes 1044480 | tf_op jit(solution)/shard_map/all_gather | solution.py:443
  60.3 7.0 collective-permute-done.2
  69.4 14.4 %collective-permute-done.10 = bf16[1000,256]{1,0:T(8,128)(2,1)} collective-permute-done((bf16[1000,256]{1,0:T(8,128)(2,1)}, bf16[1000,256]{1,0:T(8,128)(2,1)}, u32[]{:S(2)}, u32[]{:S(2)}) %collective-permute-start.10) | collective-permute-done | bytes 512032 | tf_op jit(solution)/shard_map/ppermute | solution.py:289
  101.3 3.8 convolution_convert_fusion.3.refs_2_.refs_3_.refs_4_
  106.7 10.8 %self_forward.2 = (bf16[1024,256]{1,0:T(8,128)(2,1)S(1)}, bf16[1024,256]{1,0:T(8,128)(2,1)S(1)}, f32[4,1,1024]{2,1,0:T(1,128)S(1)}) custom-call(s32[1]{0:T(128)S(6)} %select_n.422.refs_0_, f32[4,1,2048]{2,1,0:T(1,128)S(1)} %reshape.242.refs_1_, bf16[1024,768]{1,0:T(8,128)(2,1)S(1)} %convolution_convert_fusion.3.refs_2_.refs_3_.refs_4_, ...), custom_call_target="tpu_custom_call" | custom-call | flops 2147483648 | bytes 2097152 | tf_op jit(solution)/shard_map/self_forward/pallas_call | solution.py:191
  121.6 8.9 %collective-permute-done.8 = bf16[512,1280]{0,1:T(8,128)(2,1)} collective-permute-done((bf16[512,1280]{0,1:T(8,128)(2,1)}, bf16[512,1280]{0,1:T(8,128)(2,1)}, u32[]{:S(2)}, u32[]{:S(2)}) %collective-permute-start.8) | collective-permute-done | bytes 1310752 | tf_op jit(solution)/shard_map/ppermute | solution.py:289
  132.0 10.8 %self_forward.3 = (bf16[1024,256]{1,0:T(8,128)(2,1)S(1)}, bf16[1024,256]{1,0:T(8,128)(2,1)S(1)}, f32[4,1,1024]{2,1,0:T(1,128)S(1)}) custom-call(s32[1]{0:T(128)S(6)} %select_n.422.refs_0_, f32[4,1,2048]{2,1,0:T(1,128)S(1)} %reshape.249.refs_1_, bf16[1024,768]{1,0:T(8,128)(2,1)S(1)} %convolution_convert_fusion.2.refs_2_.refs_3_.refs_4_, ...), custom_call_target="tpu_custom_call" | custom-call | flops 2147483648 | bytes 2097152 | tf_op jit(solution)/shard_map/self_forward/pallas_call | solution.py:191
  145.3 3.6 select_n.440
  148.9 3.6 select_n.438
  158.8 11.4 %collective-permute-done.9 = bf16[512,1280]{0,1:T(8,128)(2,1)} collective-permute-done((bf16[512,1280]{0,1:T(8,128)(2,1)}, bf16[512,1280]{0,1:T(8,128)(2,1)}, u32[]{:S(2)}, u32[]{:S(2)}) %collective-permute-start.9) | collective-permute-done | bytes 1310752 | tf_op jit(solution)/shard_map/ppermute | solution.py:295
  173.6 3.5 select_n.446
  177.1 3.6 select_n.444
  188.4 4.0 convert_element_type.293
  208.4 11.6 %cross_forward.2 = (bf16[1024,256]{1,0:T(8,128)(2,1)S(1)}, bf16[1024,256]{1,0:T(8,128)(2,1)S(1)}, f32[4,1,1024]{2,1,0:T(1,128)S(1)}) custom-call(bf16[1024,256]{1,0:T(8,128)(2,1)S(1)} %convolution_convert_fusion.19.refs_0_, bf16[1024,512]{1,0:T(8,128)(2,1)S(1)} %convolution_convert_fusion.7.refs_1_.refs_2_, ...), custom_call_target="tpu_custom_call" | custom-call | flops 2147483648 | bytes 2097152 | tf_op jit(solution)/shard_map/cross_forward/pallas_call | solution.py:191
  220.1 11.3 %cross_forward.3 = (bf16[1024,256]{1,0:T(8,128)(2,1)S(1)}, bf16[1024,256]{1,0:T(8,128)(2,1)S(1)}, f32[4,1,1024]{2,1,0:T(1,128)S(1)}) custom-call(bf16[1024,256]{1,0:T(8,128)(2,1)S(1)} %convolution_convert_fusion.18.refs_0_, bf16[1024,512]{1,0:T(8,128)(2,1)S(1)} %convolution_convert_fusion.6.refs_1_.refs_2_, ...), custom_call_target="tpu_custom_call" | custom-call | flops 2147483648 | bytes 2097152 | tf_op jit(solution)/shard_map/cross_forward/pallas_call | solution.py:191
  234.2 8.8 %collective-permute-done.13 = bf16[512,2048]{0,1:T(8,128)(2,1)S(1)} collective-permute-done((bf16[512,2048]{0,1:T(8,128)(2,1)}, bf16[512,2048]{0,1:T(8,128)(2,1)S(1)}, u32[]{:S(2)}, u32[]{:S(2)}) %collective-permute-start.13) | collective-permute-done | bytes 2097184 | tf_op jit(solution)/shard_map/ppermute | solution.py:295
  252.1 4.0 select_n.469
  256.1 4.0 select_n.467
  261.4 4.3 pad_maximum_fusion
  272.9 10.2 %multiply_reduce_fusion.2 = (f32[1024]{0:T(1024)S(1)}, f32[1024,1024]{1,0:T(8,128)}, f32[1024,1024]{1,0:T(8,128)}) fusion(f32[1024,1024]{1,0:T(8,128)} %copy-done.18, f32[1024,1024]{1,0:T(8,128)} %copy-done.22, bf16[1024,1024]{1,0:T(8,128)(2,1)} %collective-permute-done.16, f32[1024,1024]{1,0:T(8,128)} %convolution_add_fusion.3, ...), kind=kLoop, calls=%fused_computation.64 | loop fusion | flops 8387584 | bytes 25169920 | tf_op jit(solution)/shard_map/reduce_sum | solution.py:381
  289.6 4.9 fusion.17
  294.6 16.8 %collective-permute-done.17 = bf16[512,1024]{1,0:T(8,128)(2,1)S(1)} collective-permute-done((bf16[512,1024]{1,0:T(8,128)(2,1)S(1)}, bf16[512,1024]{1,0:T(8,128)(2,1)S(1)}, u32[]{:S(2)}, u32[]{:S(2)}) %collective-permute-start.17) | collective-permute-done | bytes 1048608 | tf_op jit(solution)/shard_map/ppermute | solution.py:289
  314.5 4.3 fusion.53
  321.4 5.2 fusion.24
  326.6 4.8 fusion.119
  334.0 5.2 add_convert_fusion.1
  339.3 4.1 fusion.42
  349.6 4.7 fusion.51
  354.2 17.9 %collective-permute-done.21 = bf16[512,1024]{1,0:T(8,128)(2,1)S(1)} collective-permute-done((bf16[512,1024]{1,0:T(8,128)(2,1)S(1)}, bf16[512,1024]{1,0:T(8,128)(2,1)S(1)}, u32[]{:S(2)}, u32[]{:S(2)}) %collective-permute-start.21) | collective-permute-done | bytes 1048608 | tf_op jit(solution)/shard_map/ppermute | solution.py:289
  381.3 6.5 copy.138
  398.9 16.5 %cross_backward.3 = (bf16[1024,256]{1,0:T(8,128)(2,1)S(1)}, bf16[1024,256]{1,0:T(8,128)(2,1)S(1)}, bf16[1024,256]{1,0:T(8,128)(2,1)S(1)}) custom-call(bf16[1024,256]{1,0:T(8,128)(2,1)S(1)} %convolution_convert_fusion.18.refs_0_, bf16[1024,512]{1,0:T(8,128)(2,1)S(1)} %copy-done.13, bf16[1024,512]{1,0:T(8,128)(2,1)S(1)} %copy-done.13, ...), custom_call_target="tpu_custom_call" | custom-call | flops 5368709120 | bytes 4194304 | tf_op jit(solution)/shard_map/cross_backward/pallas_call | solution.py:254
  418.8 17.0 %cross_backward.2 = (bf16[1024,256]{1,0:T(8,128)(2,1)S(1)}, bf16[1024,256]{1,0:T(8,128)(2,1)S(1)}, bf16[1024,256]{1,0:T(8,128)(2,1)S(1)}) custom-call(bf16[1024,256]{1,0:T(8,128)(2,1)S(1)} %copy-done.3, bf16[1024,512]{1,0:T(8,128)(2,1)S(1)} %copy-done.11, bf16[1024,512]{1,0:T(8,128)(2,1)S(1)} %copy-done.11, bf16[1024,256]{1,0:T(8,128)(2,1)S(1)} %copy-done.1, ...), custom_call_target="tpu_custom_call" | custom-call | flops 5368709120 | bytes 4194304 | tf_op jit(solution)/shard_map/cross_backward/pallas_call | solution.py:254
  435.9 3.5 convolution_add_fusion
  459.2 19.4 %collective-permute-done.25 = bf16[2,1024,256]{2,1,0:T(8,128)(2,1)S(1)} collective-permute-done((bf16[2,1024,256]{2,1,0:T(8,128)(2,1)S(1)}, bf16[2,1024,256]{2,1,0:T(8,128)(2,1)S(1)}, u32[]{:S(2)}, u32[]{:S(2)}) %collective-permute-start.25) | collective-permute-done | bytes 1048608 | tf_op jit(solution)/shard_map/ppermute | solution.py:289
  496.0 4.4 fusion.9
  500.4 23.2 %collective-permute-done.27 = bf16[1024,1024]{0,1:T(8,128)(2,1)} collective-permute-done((bf16[1024,1024]{0,1:T(8,128)(2,1)}, bf16[1024,1024]{0,1:T(8,128)(2,1)}, u32[]{:S(2)}, u32[]{:S(2)}) %collective-permute-start.27) | collective-permute-done | bytes 2097184 | tf_op jit(solution)/shard_map/ppermute | solution.py:289
  525.4 14.7 %self_backward.2 = (bf16[1024,256]{1,0:T(8,128)(2,1)S(1)}, bf16[1024,256]{1,0:T(8,128)(2,1)S(1)}, bf16[1024,256]{1,0:T(8,128)(2,1)S(1)}, f32[4,8,2048]{2,1,0:T(8,128)S(1)}) custom-call(s32[1]{0:T(128)S(6)} %select_n.422.refs_0_, f32[4,1,2048]{2,1,0:T(1,128)S(1)} %reshape.254.refs_1_, bf16[1024,768]{1,0:T(8,128)(2,1)S(1)} %copy-done.7, ...), custom_call_target="tpu_custom_call" | custom-call | flops 5368709120 | bytes 4194304 | tf_op jit(solution)/shard_map/self_backward/pallas_call | solution.py:254
  550.3 14.9 %self_backward.3 = (bf16[1024,256]{1,0:T(8,128)(2,1)S(1)}, bf16[1024,256]{1,0:T(8,128)(2,1)S(1)}, bf16[1024,256]{1,0:T(8,128)(2,1)S(1)}, f32[4,8,2048]{2,1,0:T(8,128)S(1)}) custom-call(s32[1]{0:T(128)S(6)} %select_n.422.refs_0_, f32[4,1,2048]{2,1,0:T(1,128)S(1)} %reshape.255.refs_1_, bf16[1024,768]{1,0:T(8,128)(2,1)S(1)} %copy-done.5, ...), custom_call_target="tpu_custom_call" | custom-call | flops 5368709120 | bytes 4194304 | tf_op jit(solution)/shard_map/self_backward/pallas_call | solution.py:254
  565.5 3.9 add_convert_fusion
  577.2 3.8 fusion.161
  581.0 9.6 %collective-permute-done.29 = bf16[1024,256]{1,0:T(8,128)(2,1)} collective-permute-done((bf16[1024,256]{1,0:T(8,128)(2,1)}, bf16[1024,256]{1,0:T(8,128)(2,1)}, u32[]{:S(2)}, u32[]{:S(2)}) %collective-permute-start.29) | collective-permute-done | bytes 524320 | tf_op jit(solution)/shard_map/ppermute | solution.py:289
  600.5 4.5 fusion.160
  606.2 4.0 copy.136
  614.1 9.6 %collective-permute-done.39 = bf16[512,1024]{1,0:T(8,128)(2,1)} collective-permute-done((bf16[512,1024]{1,0:T(8,128)(2,1)}, bf16[512,1024]{1,0:T(8,128)(2,1)}, u32[]{:S(2)}, u32[]{:S(2)}) %collective-permute-start.39) | collective-permute-done | bytes 1048608 | tf_op jit(solution)/shard_map/ppermute | solution.py:295
  638.9 11.6 %collective-permute-done.40 = bf16[2,128,1024]{1,2,0:T(8,128)(2,1)} collective-permute-done((bf16[2,128,1024]{1,2,0:T(8,128)(2,1)}, bf16[2,128,1024]{1,2,0:T(8,128)(2,1)}, u32[]{:S(2)}, u32[]{:S(2)}) %collective-permute-start.40) | collective-permute-done | bytes 524320 | tf_op jit(solution)/shard_map/ppermute | solution.py:298
  654.5 4.2 fusion.5
  658.9 4.2 collective-permute-done.41
  672.1 4.8 fusion.28
  (618 shorter events, 265.2 us)
Async XLA Ops:
  7.3 92.5 %all-gather.3.cloned.1.call-start = ((), (), s32[]{:S(2)}) async-start(), calls=%async_computation.2 | async-start | bytes 1638400 | tf_op jit(solution)/shard_map/all_gather | solution.py:443
  13.3 175.1 %all-gather.5.cloned.1.call-start = ((), (), s32[]{:S(2)}) async-start(), calls=%async_computation.3 | async-start | bytes 2621440 | tf_op jit(solution)/shard_map/all_gather | solution.py:443
  43.9 46.4 %collective-permute-start.4 = (bf16[544,768]{1,0:T(8,128)(2,1)}, bf16[544,768]{1,0:T(8,128)(2,1)}, u32[]{:S(2)}, u32[]{:S(2)}) collective-permute-start(bf16[544,768]{1,0:T(8,128)(2,1)} %all_gather.9), channel_id=1, source_target_pairs={{0,16},{16,0},{1,17},{17,1},{2,18},{18,2},{3,19},{19,3},{4,20},{20... | collective-permute-start | bytes 2506760 | tf_op jit(solution)/shard_map/ppermute | solution.py:295
  45.5 43.5 %collective-permute-start.6 = (bf16[544,768]{1,0:T(8,128)(2,1)}, bf16[544,768]{1,0:T(8,128)(2,1)}, u32[]{:S(2)}, u32[]{:S(2)}) collective-permute-start(bf16[544,768]{1,0:T(8,128)(2,1)} %all_gather.9), channel_id=1, source_target_pairs={{0,2},{1,3},{2,0},{3,1},{4,6},{5,7},{6,4},{7,5},{8,10},{9,11},{10,... | collective-permute-start | bytes 2506760 | tf_op jit(solution)/shard_map/ppermute | solution.py:289
  47.0 20.3 %collective-permute-start.2 = (f32[3,256]{1,0:T(4,128)S(1)}, f32[3,256]{1,0:T(4,128)S(1)}, u32[]{:S(2)}, u32[]{:S(2)}) collective-permute-start(f32[3,256]{1,0:T(4,128)S(1)} %pad_maximum_fusion.35), channel_id=1, source_target_pairs={{0,2},{1,3},{2,0},{3,1},{4,6},{5,7},{6,4},{7,5},{8,10},{9,11},{10,... | collective-permute-start | bytes 9224 | tf_op jit(solution)/shard_map/ppermute | solution.py:289
  49.3 36.8 %collective-permute-start = (bf16[1024,256]{1,0:T(8,128)(2,1)S(1)}, bf16[1024,256]{1,0:T(8,128)(2,1)}, u32[]{:S(2)}, u32[]{:S(2)}) collective-permute-start(bf16[1024,256]{1,0:T(8,128)(2,1)S(1)} %select_bitcast_fusion.2), channel_id=1, source_target_pairs={{0,2},{1,3},{2,0},{3,1},{4,6},{5,7},{6,4},{7,5},{8,10},{9,11},{10,... | collective-permute-start | bytes 1572872 | tf_op jit(solution)/shard_map/ppermute | solution.py:289
  53.5 30.4 %collective-permute-start.10 = (bf16[1000,256]{1,0:T(8,128)(2,1)}, bf16[1000,256]{1,0:T(8,128)(2,1)}, u32[]{:S(2)}, u32[]{:S(2)}) collective-permute-start(bf16[1000,256]{1,0:T(8,128)(2,1)} %select_bitcast_fusion.3), channel_id=1, source_target_pairs={{0,2},{1,3},{2,0},{3,1},{4,6},{5,7},{6,4},{7,5},{8,10},{9,11},{10,... | collective-permute-start | bytes 1536008 | tf_op jit(solution)/shard_map/ppermute | solution.py:289
  57.7 578.0 %reduce-scatter.9.cloned.1.call-start = ((), (), s32[]{:S(2)}) async-start(), calls=%async_computation.5 | async-start | bytes 4718592
  67.3 2.0 collective-permute-start.3
  69.4 135.0 %copy-start.103 = (f32[1,1024]{1,0:T(1,128)}, f32[1,1024]{1,0:T(1,128)S(1)}, u32[]{:S(2)}) copy-start(f32[1,1024]{1,0:T(1,128)S(1)} %get-tuple-element.264) | copy-start | bytes 12292
  86.2 7.5 %collective-permute-start.11 = (bf16[2,1000,256]{2,1,0:T(8,128)(2,1)}, bf16[2,1000,256]{2,1,0:T(8,128)(2,1)}, u32[]{:S(2)}, u32[]{:S(2)}) collective-permute-start(bf16[2,1000,256]{2,1,0:T(8,128)(2,1)} %pad_maximum_fusion.21), channel_id=1, source_target_pairs={{0,1},{1,0},{2,3},{3,2},{4,5},{5,4},{6,7},{7,6},{8,9},{9,8},{10,11... | collective-permute-start | bytes 3072008 | tf_op jit(solution)/shard_map/ppermute | solution.py:292
  88.4 9.2 %collective-permute-start.1 = (bf16[2,1024,256]{2,1,0:T(8,128)(2,1)}, bf16[2,1024,256]{2,1,0:T(8,128)(2,1)}, u32[]{:S(2)}, u32[]{:S(2)}) collective-permute-start(bf16[2,1024,256]{2,1,0:T(8,128)(2,1)} %pad_maximum_fusion.16), channel_id=1, source_target_pairs={{0,1},{1,0},{2,3},{3,2},{4,5},{5,4},{6,7},{7,6},{8,9},{9,8},{10,11... | collective-permute-start | bytes 3145736 | tf_op jit(solution)/shard_map/ppermute | solution.py:292
  93.1 24.4 %collective-permute-start.7 = (bf16[544,768]{1,0:T(8,128)(2,1)}, bf16[544,768]{1,0:T(8,128)(2,1)}, u32[]{:S(2)}, u32[]{:S(2)}) collective-permute-start(bf16[544,768]{1,0:T(8,128)(2,1)} %collective-permute-done.6), channel_id=1, source_target_pairs={{0,16},{16,0},{1,17},{17,1},{2,18},{18,2},{3,19},{19,3},{4,20},{20... | collective-permute-start | bytes 2506760 | tf_op jit(solution)/shard_map/ppermute | solution.py:295
  99.1 101.2 %copy-start.26 = (bf16[1024,256]{1,0:T(8,128)(2,1)}, bf16[1024,256]{1,0:T(8,128)(2,1)S(1)}, u32[]{:S(2)}) copy-start(bf16[1024,256]{1,0:T(8,128)(2,1)S(1)} %get-tuple-element.231) | copy-start | bytes 1572868
  99.7 30.8 %collective-permute-start.8 = (bf16[512,1280]{0,1:T(8,128)(2,1)}, bf16[512,1280]{0,1:T(8,128)(2,1)}, u32[]{:S(2)}, u32[]{:S(2)}) collective-permute-start(bf16[512,1280]{0,1:T(8,128)(2,1)} %all-gather.3.cloned.1.call-done), channel_id=1, source_target_pairs={{0,2},{1,3},{2,0},{3,1},{4,6},{5,7},{6,4},{7,5},{8,10},{9,11},{10,... | collective-permute-start | bytes 3932168 | tf_op jit(solution)/shard_map/ppermute | solution.py:289
  105.2 38.5 %collective-permute-start.5 = (bf16[512,1280]{0,1:T(8,128)(2,1)S(1)}, bf16[512,1280]{0,1:T(8,128)(2,1)S(1)}, u32[]{:S(2)}, u32[]{:S(2)}) collective-permute-start(bf16[512,1280]{0,1:T(8,128)(2,1)S(1)} %copy-done.91), channel_id=1, source_target_pairs={{0,16},{16,0},{1,17},{17,1},{2,18},{18,2},{3,19},{19,3},{4,20},{20... | collective-permute-start | bytes 3932168 | tf_op jit(solution)/shard_map/ppermute | solution.py:295
  130.5 39.7 %collective-permute-start.9 = (bf16[512,1280]{0,1:T(8,128)(2,1)}, bf16[512,1280]{0,1:T(8,128)(2,1)}, u32[]{:S(2)}, u32[]{:S(2)}) collective-permute-start(bf16[512,1280]{0,1:T(8,128)(2,1)} %collective-permute-done.8), channel_id=1, source_target_pairs={{0,16},{16,0},{1,17},{17,1},{2,18},{18,2},{3,19},{19,3},{4,20},{20... | collective-permute-start | bytes 3932168 | tf_op jit(solution)/shard_map/ppermute | solution.py:295
  192.4 7.9 %collective-permute-start.12 = (bf16[1024,1024]{1,0:T(8,128)(2,1)}, bf16[1024,1024]{1,0:T(8,128)(2,1)}, u32[]{:S(2)}, u32[]{:S(2)}) collective-permute-start(bf16[1024,1024]{1,0:T(8,128)(2,1)} %convert_element_type.293), channel_id=1, source_target_pairs={{0,1},{1,0},{2,3},{3,2},{4,5},{5,4},{6,7},{7,6},{8,9},{9,8},{10,11... | collective-permute-start | bytes 6291464 | tf_op jit(solution)/shard_map/ppermute | solution.py:292
  193.5 40.7 %collective-permute-start.14 = (bf16[2,1024,256]{2,1,0:T(8,128)(2,1)}, bf16[2,1024,256]{2,1,0:T(8,128)(2,1)}, u32[]{:S(2)}, u32[]{:S(2)}) collective-permute-start(bf16[2,1024,256]{2,1,0:T(8,128)(2,1)} %convert_element_type.273), channel_id=1, source_target_pairs={{0,2},{1,3},{2,0},{3,1},{4,6},{5,7},{6,4},{7,5},{8,10},{9,11},{10,... | collective-permute-start | bytes 3145736 | tf_op jit(solution)/shard_map/ppermute | solution.py:289
  195.0 48.0 %collective-permute-start.13 = (bf16[512,2048]{0,1:T(8,128)(2,1)}, bf16[512,2048]{0,1:T(8,128)(2,1)S(1)}, u32[]{:S(2)}, u32[]{:S(2)}) collective-permute-start(bf16[512,2048]{0,1:T(8,128)(2,1)} %all-gather.5.cloned.1.call-done), channel_id=1, source_target_pairs={{0,16},{16,0},{1,17},{17,1},{2,18},{18,2},{3,19},{19,3},{4,20},{20... | collective-permute-start | bytes 6291464 | tf_op jit(solution)/shard_map/ppermute | solution.py:295
  244.7 28.2 %collective-permute-start.16 = (bf16[1024,1024]{1,0:T(8,128)(2,1)}, bf16[1024,1024]{1,0:T(8,128)(2,1)}, u32[]{:S(2)}, u32[]{:S(2)}) collective-permute-start(bf16[1024,1024]{1,0:T(8,128)(2,1)} %convert_element_type.300), channel_id=1, source_target_pairs={{0,1},{1,0},{2,3},{3,2},{4,5},{5,4},{6,7},{7,6},{8,9},{9,8},{10,11... | collective-permute-start | bytes 6291464 | tf_op jit(solution)/shard_map/ppermute | solution.py:292
  249.2 19.6 %collective-permute-start.18 = (bf16[2,1024,256]{2,1,0:T(8,128)(2,1)}, bf16[2,1024,256]{2,1,0:T(8,128)(2,1)}, u32[]{:S(2)}, u32[]{:S(2)}) collective-permute-start(bf16[2,1024,256]{2,1,0:T(8,128)(2,1)} %pad_maximum_fusion.18), channel_id=1, source_target_pairs={{0,1},{1,0},{2,3},{3,2},{4,5},{5,4},{6,7},{7,6},{8,9},{9,8},{10,11... | collective-permute-start | bytes 3145736 | tf_op jit(solution)/shard_map/ppermute | solution.py:292
  261.2 9.2 %collective-permute-start.15 = (bf16[2,1024,256]{2,1,0:T(8,128)(2,1)S(1)}, bf16[2,1024,256]{2,1,0:T(8,128)(2,1)S(1)}, u32[]{:S(2)}, u32[]{:S(2)}) collective-permute-start(bf16[2,1024,256]{2,1,0:T(8,128)(2,1)S(1)} %pad_maximum_fusion.17), channel_id=1, source_target_pairs={{0,1},{1,0},{2,3},{3,2},{4,5},{5,4},{6,7},{7,6},{8,9},{9,8},{10,11... | collective-permute-start | bytes 3145736 | tf_op jit(solution)/shard_map/ppermute | solution.py:292
  285.9 25.5 %collective-permute-start.17 = (bf16[512,1024]{1,0:T(8,128)(2,1)S(1)}, bf16[512,1024]{1,0:T(8,128)(2,1)S(1)}, u32[]{:S(2)}, u32[]{:S(2)}) collective-permute-start(bf16[512,1024]{1,0:T(8,128)(2,1)S(1)} %constant_dynamic-slice_fusion.7), channel_id=1, source_target_pairs={{0,2},{1,3},{2,0},{3,1},{4,6},{5,7},{6,4},{7,5},{8,10},{9,11},{10,... | collective-permute-start | bytes 3145736 | tf_op jit(solution)/shard_map/ppermute | solution.py:289
  311.4 7.4 %collective-permute-start.19 = (bf16[512,1024]{1,0:T(8,128)(2,1)S(1)}, bf16[512,1024]{1,0:T(8,128)(2,1)S(1)}, u32[]{:S(2)}, u32[]{:S(2)}) collective-permute-start(bf16[512,1024]{1,0:T(8,128)(2,1)S(1)} %collective-permute-done.17), channel_id=1, source_target_pairs={{0,1},{1,0},{2,3},{3,2},{4,5},{5,4},{6,7},{7,6},{8,9},{9,8},{10,11... | collective-permute-start | bytes 3145736 | tf_op jit(solution)/shard_map/ppermute | solution.py:292
  313.9 58.2 %collective-permute-start.23 = (bf16[512,1024]{1,0:T(8,128)(2,1)S(1)}, bf16[512,1024]{1,0:T(8,128)(2,1)S(1)}, u32[]{:S(2)}, u32[]{:S(2)}) collective-permute-start(bf16[512,1024]{1,0:T(8,128)(2,1)S(1)} %dynamic-slice_convert_fusion), channel_id=1, source_target_pairs={{0,1},{1,0},{2,3},{3,2},{4,5},{5,4},{6,7},{7,6},{8,9},{9,8},{10,11... | collective-permute-start | bytes 3145736 | tf_op jit(solution)/shard_map/ppermute | solution.py:292
  333.9 12.0 %collective-permute-start.20 = (bf16[512,1024]{1,0:T(8,128)(2,1)S(1)}, bf16[512,1024]{1,0:T(8,128)(2,1)S(1)}, u32[]{:S(2)}, u32[]{:S(2)}) collective-permute-start(bf16[512,1024]{1,0:T(8,128)(2,1)S(1)} %dynamic-slice_convert_fusion.1), channel_id=1, source_target_pairs={{0,1},{1,0},{2,3},{3,2},{4,5},{5,4},{6,7},{7,6},{8,9},{9,8},{10,11... | collective-permute-start | bytes 3145736 | tf_op jit(solution)/shard_map/ppermute | solution.py:292
  346.5 25.6 %collective-permute-start.21 = (bf16[512,1024]{1,0:T(8,128)(2,1)S(1)}, bf16[512,1024]{1,0:T(8,128)(2,1)S(1)}, u32[]{:S(2)}, u32[]{:S(2)}) collective-permute-start(bf16[512,1024]{1,0:T(8,128)(2,1)S(1)} %add_convert_fusion.4), channel_id=1, source_target_pairs={{0,2},{1,3},{2,0},{3,1},{4,6},{5,7},{6,4},{7,5},{8,10},{9,11},{10,... | collective-permute-start | bytes 3145736 | tf_op jit(solution)/shard_map/ppermute | solution.py:289
  373.6 14.2 %collective-permute-start.24 = (bf16[512,1024]{1,0:T(8,128)(2,1)}, bf16[512,1024]{1,0:T(8,128)(2,1)}, u32[]{:S(2)}, u32[]{:S(2)}) collective-permute-start(bf16[512,1024]{1,0:T(8,128)(2,1)} %add_convert_fusion.3), channel_id=1, source_target_pairs={{0,1},{1,0},{2,3},{3,2},{4,5},{5,4},{6,7},{7,6},{8,9},{9,8},{10,11... | collective-permute-start | bytes 3145736 | tf_op jit(solution)/shard_map/ppermute | solution.py:292
  380.4 66.9 %collective-permute-start.22 = (bf16[4096,256]{1,0:T(8,128)(2,1)}, bf16[4096,256]{1,0:T(8,128)(2,1)}, u32[]{:S(2)}, u32[]{:S(2)}) collective-permute-start(bf16[4096,256]{1,0:T(8,128)(2,1)} %pad_maximum_fusion.8), channel_id=1, source_target_pairs={{0,1},{1,0},{2,3},{3,2},{4,5},{5,4},{6,7},{7,6},{8,9},{9,8},{10,11... | collective-permute-start | bytes 6291464 | tf_op jit(solution)/shard_map/ppermute | solution.py:292
  387.8 296.9 %reduce-scatter.7.cloned.1.call-start = ((), (), s32[]{:S(2)}) async-start(), calls=%async_computation.4 | async-start | bytes 2359296
  440.9 42.8 %collective-permute-start.30 = (bf16[2048,256]{1,0:T(8,128)(2,1)}, bf16[2048,256]{1,0:T(8,128)(2,1)S(1)}, u32[]{:S(2)}, u32[]{:S(2)}) collective-permute-start(bf16[2048,256]{1,0:T(8,128)(2,1)} %pad_maximum_fusion.20), channel_id=1, source_target_pairs={{0,1},{1,0},{2,3},{3,2},{4,5},{5,4},{6,7},{7,6},{8,9},{9,8},{10,11... | collective-permute-start | bytes 3145736 | tf_op jit(solution)/shard_map/ppermute | solution.py:292
  452.5 26.1 %collective-permute-start.25 = (bf16[2,1024,256]{2,1,0:T(8,128)(2,1)S(1)}, bf16[2,1024,256]{2,1,0:T(8,128)(2,1)S(1)}, u32[]{:S(2)}, u32[]{:S(2)}) collective-permute-start(bf16[2,1024,256]{2,1,0:T(8,128)(2,1)S(1)} %pad_maximum_fusion.19), channel_id=1, source_target_pairs={{0,2},{1,3},{2,0},{3,1},{4,6},{5,7},{6,4},{7,5},{8,10},{9,11},{10,... | collective-permute-start | bytes 3145736 | tf_op jit(solution)/shard_map/ppermute | solution.py:289
  457.9 65.7 %collective-permute-start.27 = (bf16[1024,1024]{0,1:T(8,128)(2,1)}, bf16[1024,1024]{0,1:T(8,128)(2,1)}, u32[]{:S(2)}, u32[]{:S(2)}) collective-permute-start(bf16[1024,1024]{0,1:T(8,128)(2,1)} %pad_maximum_fusion.10), channel_id=1, source_target_pairs={{0,2},{1,3},{2,0},{3,1},{4,6},{5,7},{6,4},{7,5},{8,10},{9,11},{10,... | collective-permute-start | bytes 6291464 | tf_op jit(solution)/shard_map/ppermute | solution.py:289
  482.1 10.5 %collective-permute-start.26 = (bf16[1024,1024]{1,0:T(8,128)(2,1)}, bf16[1024,1024]{1,0:T(8,128)(2,1)S(1)}, u32[]{:S(2)}, u32[]{:S(2)}) collective-permute-start(bf16[1024,1024]{1,0:T(8,128)(2,1)} %get-tuple-element.283), channel_id=1, source_target_pairs={{0,1},{1,0},{2,3},{3,2},{4,5},{5,4},{6,7},{7,6},{8,9},{9,8},{10,11... | collective-permute-start | bytes 6291464 | tf_op jit(solution)/shard_map/ppermute | solution.py:292
  485.9 95.1 %collective-permute-start.31 = (bf16[1000,256]{1,0:T(8,128)(2,1)}, bf16[1000,256]{1,0:T(8,128)(2,1)}, u32[]{:S(2)}, u32[]{:S(2)}) collective-permute-start(bf16[1000,256]{1,0:T(8,128)(2,1)} %fusion.80), channel_id=1, source_target_pairs={{0,2},{1,3},{2,0},{3,1},{4,6},{5,7},{6,4},{7,5},{8,10},{9,11},{10,... | collective-permute-start | bytes 1536008 | tf_op jit(solution)/shard_map/ppermute | solution.py:289
  544.9 45.8 %collective-permute-start.28 = (bf16[1024,768]{1,0:T(8,128)(2,1)}, bf16[1024,768]{1,0:T(8,128)(2,1)}, u32[]{:S(2)}, u32[]{:S(2)}) collective-permute-start(bf16[1024,768]{1,0:T(8,128)(2,1)} %convolution_convert_fusion.1), channel_id=1, source_target_pairs={{0,2},{1,3},{2,0},{3,1},{4,6},{5,7},{6,4},{7,5},{8,10},{9,11},{10,... | collective-permute-start | bytes 4718600 | tf_op jit(solution)/shard_map/ppermute | solution.py:289
  547.1 43.6 %collective-permute-start.29 = (bf16[1024,256]{1,0:T(8,128)(2,1)}, bf16[1024,256]{1,0:T(8,128)(2,1)}, u32[]{:S(2)}, u32[]{:S(2)}) collective-permute-start(bf16[1024,256]{1,0:T(8,128)(2,1)} %convolution_convert_fusion.11), channel_id=1, source_target_pairs={{0,2},{1,3},{2,0},{3,1},{4,6},{5,7},{6,4},{7,5},{8,10},{9,11},{10,... | collective-permute-start | bytes 1572872 | tf_op jit(solution)/shard_map/ppermute | solution.py:289
  599.5 24.2 %collective-permute-start.39 = (bf16[512,1024]{1,0:T(8,128)(2,1)}, bf16[512,1024]{1,0:T(8,128)(2,1)}, u32[]{:S(2)}, u32[]{:S(2)}) collective-permute-start(bf16[512,1024]{1,0:T(8,128)(2,1)} %fusion.39), channel_id=1, source_target_pairs={{0,16},{16,0},{1,17},{17,1},{2,18},{18,2},{3,19},{19,3},{4,20},{20... | collective-permute-start | bytes 3145736 | tf_op jit(solution)/shard_map/ppermute | solution.py:295
  605.0 49.5 %collective-permute-start.32 = (bf16[1024,1024]{1,0:T(8,128)(2,1)}, bf16[1024,1024]{1,0:T(8,128)(2,1)}, u32[]{:S(2)}, u32[]{:S(2)}) collective-permute-start(bf16[1024,1024]{1,0:T(8,128)(2,1)} %get-tuple-element.285), channel_id=1, source_target_pairs={{0,1},{1,0},{2,3},{3,2},{4,5},{5,4},{6,7},{7,6},{8,9},{9,8},{10,11... | collective-permute-start | bytes 6291464 | tf_op jit(solution)/shard_map/ppermute | solution.py:292
  627.7 22.7 %collective-permute-start.40 = (bf16[2,128,1024]{1,2,0:T(8,128)(2,1)}, bf16[2,128,1024]{1,2,0:T(8,128)(2,1)}, u32[]{:S(2)}, u32[]{:S(2)}) collective-permute-start(bf16[2,128,1024]{1,2,0:T(8,128)(2,1)} %bitcast.229), channel_id=1, source_target_pairs={{0,4},{4,0},{8,12},{12,8},{1,5},{5,1},{9,13},{13,9},{2,6},{6,2},{1... | collective-permute-start | bytes 1572872 | tf_op jit(solution)/shard_map/ppermute | solution.py:298
  652.0 11.1 %collective-permute-start.41 = (bf16[1,128,1024]{1,2,0:T(8,128)(2,1)S(1)}, bf16[1,128,1024]{1,2,0:T(8,128)(2,1)S(1)}, u32[]{:S(2)}, u32[]{:S(2)}) collective-permute-start(bf16[1,128,1024]{1,2,0:T(8,128)(2,1)S(1)} %dynamic-slice_convert_fusion.9), channel_id=1, source_target_pairs={{0,8},{4,12},{8,0},{12,4},{1,9},{5,13},{9,1},{13,5},{2,10},{6,14},... | collective-permute-start | bytes 786440 | tf_op jit(solution)/shard_map/ppermute | solution.py:298
  658.8 4.3 collective-permute-start.34
  663.2 5.2 collective-permute-start.35
  668.4 3.7 collective-permute-start.36
  672.1 4.8 collective-permute-start.37
  676.9 4.6 collective-permute-start.38
  679.5 11.2 %collective-permute-start.33 = (bf16[1024,256]{1,0:T(8,128)(2,1)S(1)}, bf16[1024,256]{1,0:T(8,128)(2,1)S(1)}, u32[]{:S(2)}, u32[]{:S(2)}) collective-permute-start(bf16[1024,256]{1,0:T(8,128)(2,1)S(1)} %dynamic-slice_convert_fusion.2), channel_id=1, source_target_pairs={{0,2},{1,3},{2,0},{3,1},{4,6},{5,7},{6,4},{7,5},{8,10},{9,11},{10,... | collective-permute-start | bytes 1572872 | tf_op jit(solution)/shard_map/ppermute | solution.py:289
  (138 other events, 1390.9 us)
Sparse Core Ops, SparseCore 0:
  13.4 43.5 all-gather.2
  59.1 45.9 all-gather.4
  387.9 88.1 reduce-scatter.8
  610.4 74.3 reduce-scatter.6
